TPU v7x, 32 devices: a whole 2x2x4 slice. The times are simulated.
32 devices in a mesh: branch: 2 (over y), res: 16 (over z, x, core).
Axes of the slice: x: 2, y: 2, z: 4, core: 2. Of those that a mesh axis runs over, the one named last changes fastest.
Arguments:
- alignment_representation: float32 [128, 96, 256], P(None, 'res'), may hold values from -6 to 6
- pairwise_state: float32 [96, 96, 128], P('res'), may hold values from -6 to 6
- alignment_mask: int32 [128, 96], P(None, 'res'), may hold values from 0 to 1, as said below
- residue_present_mask: int32 [96], P('res'), may hold values from 0 to 1, as said below
- row_projection_weight: float32 [4, 256, 256], replicated
- lateral_result_coeffs: float32 [256, 256], replicated, may hold values from -1.5 to 1.5
- pair_bias_weight: float32 [128, 8], replicated, may hold values from -0.75 to 0.75
- first_operand_coeffs: float32 [256, 32], replicated, may hold values from -0.375 to 0.375
- other_operand_coeffs: float32 [256, 32], replicated, may hold values from -0.375 to 0.375
- outer_output_weight: float32 [1024, 128], replicated, may hold values from -2 to 2
- starting_projection_weight: float32 [4, 128, 128], replicated
- starting_bias_weight: float32 [128, 4], replicated, may hold values from -0.75 to 0.75
- starting_output_weight: float32 [128, 128], replicated, may hold values from -2 to 2
- ending_projection_weight: float32 [4, 128, 128], replicated
- ending_bias_weight: float32 [128, 4], replicated, may hold values from -0.75 to 0.75
- ending_output_weight: float32 [128, 128], replicated, may hold values from -2 to 2
Outputs:
- alignment_output: float32 [128, 96, 256], P('branch', 'res')
- pairwise_output: float32 [96, 96, 128], P('res', None, 'branch')
Inputs may be any that keep to these rules, and one draw needn't show every extreme that they name: residue_present_mask is 1 on the first L residues and 0 on the rest, for a drawn L from 48 to 96. alignment_mask[s, r] is 1 exactly where s is below a drawn count from 32 to 128 and residue_present_mask[r] is 1.
All inputs are finite; a program needn't handle non-finite values.
Results may differ from a plain program's by a relative error of at most 0.0003.
Values sent between devices are 32-bit elements; how exact they have to be, the bound alone decides.
A program may use at most 128 MiB of HBM per device.

v0:
```python
import math

import jax
import jax.numpy as jnp
from jax import lax
from jax.sharding import PartitionSpec as P

ATTEND_HEADS = 8
HEADS_Z = 4


highest = lax.Precision.HIGHEST
epsilon = 1e-05
masked_score = -1000000000.0


def spread(value, axis, root):
    mine = lax.axis_index(axis) == root
    return lax.psum(jnp.where(mine, value, jnp.zeros_like(value)), axis)


def partner(block, axis, apart):
    count = lax.axis_size(axis)
    route = []
    for low in range(count):
        high = low | 1 << apart
        if high != low and high < count:
            route += [(low, high), (high, low)]
    return lax.ppermute(block, axis, route)


def layer_normalize(values):
    centred = values - jnp.mean(values, axis=-1, keepdims=True)
    variance = jnp.mean(centred * centred, axis=-1, keepdims=True)
    return centred * lax.rsqrt(variance + epsilon)


def linear_project(values, weight):
    return jnp.dot(values, weight, precision=highest, preferred_element_type=jnp.float32)


def attend(query_matrix, key_matrix, value_matrix, gate_matrix, score_bias, live_keys, head_count):
    head_width = query_matrix.shape[-1] // head_count
    shaped_q = query_matrix.reshape(query_matrix.shape[0], head_count, head_width)
    shaped_k = key_matrix.reshape(key_matrix.shape[0], head_count, head_width)
    shaped_v = value_matrix.reshape(value_matrix.shape[0], head_count, head_width)
    scores = (
        jnp.einsum("qhd,khd->hqk", shaped_q, shaped_k, precision=highest) / math.sqrt(head_width)
        + score_bias
    )
    scores = jnp.where(live_keys[None, None, :], scores, masked_score)
    scores = scores - jnp.max(scores, axis=-1, keepdims=True)
    weights = jnp.exp(scores)
    weights = weights / jnp.sum(weights, axis=-1, keepdims=True)
    mixture = jnp.einsum("hqk,khd->qhd", weights, shaped_v, precision=highest)
    return jax.nn.sigmoid(gate_matrix) * mixture.reshape(
        query_matrix.shape[0], head_count * head_width
    )


def factor_matrix(normed, float_mask, weight):
    return jnp.transpose(linear_project(normed, weight) * float_mask[:, :, None], (1, 2, 0))


def outer_block(left_matrix, mask_rows, right_all, mask_all, out_weight):
    residues, factor_width, sequences = right_all.shape

    def outer_one_row(operands):
        row_left, row_mask = operands
        outer_sum = jnp.einsum("cs,jes->jce", row_left, right_all, precision=highest)
        outer_sum = outer_sum.reshape(residues, factor_width * factor_width)
        intersection = jnp.einsum("ns,s->n", mask_all, row_mask, precision=highest)
        return linear_project(outer_sum, out_weight) / jnp.maximum(intersection, 1.0)[:, None]

    return lax.map(outer_one_row, (left_matrix, mask_rows))


def per_device(
    alignment_representation,
    pairwise_state,
    alignment_mask,
    residue_present_mask,
    row_projection_weight,
    lateral_result_coeffs,
    pair_bias_weight,
    first_operand_coeffs,
    other_operand_coeffs,
    outer_output_weight,
    starting_projection_weight,
    starting_bias_weight,
    starting_output_weight,
    ending_projection_weight,
    ending_bias_weight,
    ending_output_weight,
):
    alignment_present_flag = lax.axis_index("branch") == 0
    sequence_count = alignment_representation.shape[0]
    local_matrix = alignment_representation.shape[1]
    residues = pairwise_state.shape[1]
    pair_width = pairwise_state.shape[2]
    float_mask = alignment_mask.astype(jnp.float32)
    mask_rows = jnp.transpose(float_mask)
    update_dimensions = (local_matrix, residues, pair_width)

    def bias_rows_of(field):
        return jnp.einsum(
            "ijc,ch->hij", layer_normalize(field), pair_bias_weight, precision=highest
        )

    normed_alignment = layer_normalize(alignment_representation)
    handed = lax.cond(
        alignment_present_flag,
        lambda: jnp.zeros((pair_bias_weight.shape[1], local_matrix, residues), jnp.float32),
        lambda: bias_rows_of(pairwise_state),
    )
    own_rows = spread(handed, "branch", 1)
    row_bias = lax.all_gather(own_rows, "res", axis=1, tiled=True)
    seq_normed, seq_mask = (
        lax.all_to_all(normed_alignment, "res", split_axis=0, concat_axis=1, tiled=True),
        lax.all_to_all(float_mask, "res", split_axis=0, concat_axis=1, tiled=True),
    )

    def row_attention():
        query_matrix = linear_project(seq_normed, row_projection_weight[0])
        key_matrix = linear_project(seq_normed, row_projection_weight[1])
        value_matrix = linear_project(seq_normed, row_projection_weight[2])
        gate_matrix = linear_project(seq_normed, row_projection_weight[3])
        sequence_present = seq_mask > 0.5

        def one_sequence(operands):
            return attend(
                operands[0],
                operands[1],
                operands[2],
                operands[3],
                row_bias,
                operands[4],
                ATTEND_HEADS,
            )

        gated_output = lax.map(
            one_sequence, (query_matrix, key_matrix, value_matrix, gate_matrix, sequence_present)
        )
        return linear_project(gated_output, lateral_result_coeffs)

    row_change = lax.cond(alignment_present_flag, row_attention, lambda: jnp.zeros_like(seq_normed))
    alignment_delta = lax.all_to_all(row_change, "res", split_axis=1, concat_axis=0, tiled=True)
    alignment_result = alignment_representation + alignment_delta
    left_matrix = factor_matrix(normed_alignment, float_mask, first_operand_coeffs)
    right_matrix = factor_matrix(normed_alignment, float_mask, other_operand_coeffs)
    right_all, mask_all = (
        lax.all_gather(right_matrix, "res", axis=0, tiled=True),
        lax.all_gather(mask_rows, "res", axis=0, tiled=True),
    )
    update = lax.cond(
        alignment_present_flag,
        lambda: outer_block(left_matrix, mask_rows, right_all, mask_all, outer_output_weight),
        lambda: jnp.zeros(update_dimensions, jnp.float32),
    )
    update = spread(update, "branch", 0)
    pair_one = pairwise_state + update
    normed_one = layer_normalize(pair_one)
    start_rows = jnp.einsum("ijc,ch->hij", normed_one, starting_bias_weight, precision=highest)
    start_full, live_float = (
        lax.all_gather(start_rows, "res", axis=1, tiled=True),
        lax.all_gather(residue_present_mask.astype(jnp.float32), "res", axis=0, tiled=True),
    )
    live_keys = live_float > 0.5

    def starting():
        query_matrix = linear_project(normed_one, starting_projection_weight[0])
        key_matrix = linear_project(normed_one, starting_projection_weight[1])
        value_matrix = linear_project(normed_one, starting_projection_weight[2])
        gate_matrix = linear_project(normed_one, starting_projection_weight[3])

        def starting_one_row(operands):
            return attend(
                operands[0], operands[1], operands[2], operands[3], start_full, live_keys, HEADS_Z
            )

        gated_output = lax.map(
            starting_one_row, (query_matrix, key_matrix, value_matrix, gate_matrix)
        )
        return pair_one + linear_project(gated_output, starting_output_weight)

    pairwise_second = lax.cond(alignment_present_flag, lambda: jnp.zeros_like(pair_one), starting)
    normed_two = layer_normalize(pairwise_second)
    end_rows = jnp.einsum("ijc,ch->hij", normed_two, ending_bias_weight, precision=highest)
    end_full = lax.all_gather(end_rows, "res", axis=1, tiled=True)
    end_score = jnp.transpose(end_full, (0, 2, 1))
    normed_cols = lax.all_to_all(normed_two, "res", split_axis=1, concat_axis=0, tiled=True)
    column_shape = normed_cols.shape

    def ending():
        ending_q, ending_k, ending_v, ending_g = (
            linear_project(normed_cols, ending_projection_weight[0]),
            linear_project(normed_cols, ending_projection_weight[1]),
            linear_project(normed_cols, ending_projection_weight[2]),
            linear_project(normed_cols, ending_projection_weight[3]),
        )

        def one_column(column, buffer):
            result = attend(
                lax.dynamic_index_in_dim(ending_q, column, 1, keepdims=False),
                lax.dynamic_index_in_dim(ending_k, column, 1, keepdims=False),
                lax.dynamic_index_in_dim(ending_v, column, 1, keepdims=False),
                lax.dynamic_index_in_dim(ending_g, column, 1, keepdims=False),
                end_score,
                live_keys,
                HEADS_Z,
            )
            return lax.dynamic_update_index_in_dim(buffer, result, column, 1)

        gated_cols = lax.fori_loop(0, ending_q.shape[1], one_column, jnp.zeros_like(ending_q))
        return linear_project(gated_cols, ending_output_weight)

    ending_delta = lax.cond(
        alignment_present_flag, lambda: jnp.zeros(column_shape, jnp.float32), ending
    )
    pair_delta = lax.all_to_all(ending_delta, "res", split_axis=0, concat_axis=1, tiled=True)
    pairwise_result = pairwise_second + pair_delta
    sequence_halves = sequence_count // 2
    halved_width = pair_width // 2
    selected_alignment, selected_pairwise = partner(
        (alignment_result[sequence_halves:], pairwise_result[:, :, :halved_width]), "branch", 0
    )
    closing_alignment = jnp.where(
        alignment_present_flag, alignment_result[:sequence_halves], selected_alignment
    )
    final_pairwise = jnp.where(
        alignment_present_flag, selected_pairwise, pairwise_result[:, :, halved_width:]
    )
    return (closing_alignment, final_pairwise)


def solution(mesh):
    in_specs = (
        P(None, "res", None),
        P("res", None, None),
        P(None, "res"),
        P("res"),
        P(),
        P(),
        P(),
        P(),
        P(),
        P(),
        P(),
        P(),
        P(),
        P(),
        P(),
        P(),
    )
    out_specs = (P("branch", "res", None), P("res", None, "branch"))
    return jax.shard_map(
        per_device, mesh=mesh, in_specs=in_specs, out_specs=out_specs, check_vma=False
    )
```

profile of v0, /device:TPU:0, one launch (start us, length us, event | category | flops | bytes accessed | tf_op | source)
XLA Modules:
  0.0 355.1 jit_solution(5219426426211909906)
XLA Ops:
  7.2 1.4 reduce_sum.109
  8.8 1.8 fusion.82
  10.8 1.5 fusion.80
  12.4 2.9 fusion.79
  16.0 7.4 %all-to-all-start.1 = ((f32[16,8,6]{1,2,0:T(8,128)}), f32[16,8,6]{1,2,0:T(8,128)}, u32[]{:S(2)}, u32[]{:S(2)}) async-start(f32[16,8,6]{1,2,0:T(8,128)} %copy.256), calls=%async_computation.1 | async-start | bytes 131072 | tf_op jit(solution)/shard_map/all_to_all | solution.py:120
  24.8 21.9 %all-gather = f32[16,6,128]{2,1,0:T(8,128)S(1)} all-gather(f32[1,6,128]{2,1,0:T(8,128)S(1)} %get-tuple-element.724), channel_id=1, replica_groups=mesh['branch'=2,'res'=16] {'res'}, dimensions={0}, use_global_device_ids=true | all-gather | bytes 52224 | tf_op jit(solution)/shard_map/all_gather | solution.py:153
  46.7 2.2 convolution_bitcast_fusion.4
  48.9 8.9 %all-gather.3.cloned.1.call-done = f32[96,32,128]{2,1,0:T(8,128)} async-done(((f32[6,32,128]{2,1,0:T(8,128)}), f32[96,32,128]{2,1,0:T(8,128)}) %all-gather.3.cloned.1.call-update) | async-done | bytes 1572880 | tf_op jit(solution)/shard_map/all_gather | solution.py:152
  57.8 35.2 %conditional.7 = (f32[6,96,128]{2,1,0:T(8,128)}) conditional(s32[]{:T(128)} %convert_element_type.6, () %tuple.72, (f32[6,128]{1,0:T(8,128)S(1)}, f32[6,32,128]{2,1,0:T(8,128)S(1)}, f32[96,32,128]{2,1,0:T(8,128)}, f32[1024,128]{1,0:T(8,128)S(1)}, f32[16,6,128]{2,1,0:T(8,128)S(1)}) %tuple.207), branch_computations={%region_13.14_spmd, %region_14.17_spmd} | conditional | flops 302174304 | bytes 7230381 | solution.py:155
  57.8 2.4 copy.264
  60.2 32.8 %while.40 = (s32[]{:T(128)}, f32[6,96,128]{2,1,0:T(8,128)}, f32[6,32,128]{2,1,0:T(8,128)S(1)}, f32[96,32,128]{2,0,1:T(8,128)S(1)}, f32[1024,128]{1,0:T(8,128)S(1...) while((s32[]{:T(128)}, f32[6,96,128]{2,1,0:T(8,128)}, f32[6,32,128]{2,1,0:T(8,128)S(1)}, ...), condition=%wide.region_16.16_spmd, body=%wide.region_15.15_spmd.sunk | while | flops 302149728 | bytes 3786589 | solution.py:75
  60.2 3.3 convolution_bitcast_fusion.8
  64.0 1.7 fusion.173
  65.7 3.3 convolution_bitcast_fusion.8
  69.5 1.7 fusion.173
  71.1 3.3 convolution_bitcast_fusion.8
  74.9 1.7 fusion.173
  76.6 3.3 convolution_bitcast_fusion.8
  80.4 1.7 fusion.173
  82.1 3.3 convolution_bitcast_fusion.8
  85.8 1.7 fusion.173
  87.5 3.3 convolution_bitcast_fusion.8
  91.3 1.7 fusion.173
  93.0 1.7 broadcast_select_fusion
  94.8 31.4 %all-reduce = f32[96]{0:T(128)S(1)} all-reduce(f32[96]{0:T(128)S(1)} %convert_dynamic-update-slice_fusion), channel_id=1, replica_groups=mesh['branch'=2,'res'=16] {'res'}, use_global_device_ids=true, to_apply=%add | all-reduce | flops 96 | bytes 768
  126.2 1.1 fusion.93
  127.7 3.8 %all-to-all-start = ((f32[128,6,256]{2,1,0:T(8,128)}), f32[128,6,256]{2,1,0:T(8,128)S(1)}, u32[]{:S(2)}, u32[]{:S(2)}) async-start(f32[128,6,256]{2,1,0:T(8,128)} %fusion.80), calls=%async_computation | async-start | bytes 2097152 | tf_op jit(solution)/shard_map/all_to_all | solution.py:119
  132.4 33.2 %all_gather.22 = f32[4,96,96]{2,0,1:T(4,128)S(1)} all-gather(f32[4,6,96]{2,0,1:T(4,128)S(1)} %convolution_bitcast_fusion.6), channel_id=1, replica_groups=mesh['branch'=2,'res'=16] {'res'}, dimensions={1}, use_global_device_ids=true | all-gather | bytes 156672 | tf_op jit(solution)/shard_map/all_gather | solution.py:165
  166.3 1.0 fusion.85
  167.3 5.9 %all-to-all-start.3 = ((f32[6,96,128]{2,0,1:T(8,128)}), f32[6,96,128]{2,0,1:T(8,128)}, u32[]{:S(2)}, u32[]{:S(2)}) async-start(f32[6,96,128]{2,0,1:T(8,128)} %fusion.85), calls=%async_computation.3 | async-start | bytes 786432 | tf_op jit(solution)/shard_map/all_to_all | solution.py:191
  173.2 33.9 %psum.14 = f32[8,6,96]{2,0,1:T(8,128)S(1)} all-reduce(f32[8,6,96]{2,0,1:T(8,128)S(1)} %broadcast_select_fusion.1), channel_id=1, replica_groups=mesh['branch'=2,'res'=16] {'branch'}, use_global_device_ids=true, to_apply=%region_6.7 | all-reduce | flops 4608 | bytes 36864 | tf_op jit(solution)/shard_map/psum | solution.py:19
  207.2 22.8 %all_gather.18 = f32[8,96,96]{2,0,1:T(8,128)S(1)} all-gather(f32[8,6,96]{2,0,1:T(8,128)S(1)} %psum.14), channel_id=1, replica_groups=mesh['branch'=2,'res'=16] {'res'}, dimensions={1}, use_global_device_ids=true | all-gather | bytes 313344 | tf_op jit(solution)/shard_map/all_gather | solution.py:117
  230.0 1.1 copy.330
  231.1 53.1 %conditional.6 = (f32[8,96,256]{2,1,0:T(8,128)S(1)}) conditional(s32[]{:T(128)} %convert_element_type.6, () %tuple.68, (f32[4,256,256]{2,1,0:T(8,128)}, f32[8,16,6,256]{3,0,1,2:T(8,128)}, f32[8,16,6]{0,2,1:T(8,128)}, f32[8,96,96]{2,0,1:T(8,128)S(1)}, f32[256,256]{1,0:T(8,128)}) %tuple.209), branch_computations={%region_7.8_spmd, %region_8.13_spmd} | conditional | flops 3077209344 | bytes 19131672 | solution.py:146
  231.1 1.3 copy.257
  232.6 1.3 fusion.12
  233.9 2.3 fusion.14
  236.1 2.3 fusion.16
  238.4 2.3 fusion.18
  240.9 1.0 copy.258
  242.0 39.1 %while.39 = (s32[]{:T(128)}, f32[8,96,256]{1,2,0:T(8,128)}, f32[8,96,256]{1,2,0:T(8,128)}, f32[8,96,256]{1,2,0:T(8,128)}, pred[8,96]{1,0:T(8,128)(4,1)S(1)}, /*i...) while((s32[]{:T(128)}, f32[8,96,256]{1,2,0:T(8,128)}, ...), condition=%wide.region_12.12_spmd, body=%wide.region_9.11_spmd.sunk | while | flops 57309696 | bytes 2539401 | solution.py:141
  242.0 1.0 constant_dynamic-slice_fusion.21
  245.4 1.6 constant_dynamic-update-slice_fusion.8
  247.0 0.9 constant_dynamic-slice_fusion.21
  250.2 1.6 constant_dynamic-update-slice_fusion.8
  251.9 0.9 constant_dynamic-slice_fusion.21
  255.1 1.6 constant_dynamic-update-slice_fusion.8
  260.0 1.6 constant_dynamic-update-slice_fusion.8
  264.9 1.6 constant_dynamic-update-slice_fusion.8
  266.5 0.9 constant_dynamic-slice_fusion.21
  269.8 1.6 constant_dynamic-update-slice_fusion.8
  271.4 0.9 constant_dynamic-slice_fusion.21
  274.7 1.6 constant_dynamic-update-slice_fusion.8
  279.6 1.6 constant_dynamic-update-slice_fusion.8
  281.2 3.0 fusion.20
  284.2 1.3 copy.260
  285.6 3.7 %all-to-all-start.2 = ((f32[8,96,256]{2,0,1:T(8,128)}), f32[8,96,256]{2,0,1:T(8,128)S(1)}, u32[]{:S(2)}, u32[]{:S(2)}) async-start(f32[8,96,256]{2,0,1:T(8,128)} %copy.260), calls=%async_computation.2 | async-start | bytes 1572864 | tf_op jit(solution)/shard_map/all_to_all | solution.py:147
  289.4 1.6 convolution_bitcast_fusion.5
  291.0 28.1 %all_gather.23 = f32[4,96,96]{2,0,1:T(4,128)S(1)} all-gather(f32[4,6,96]{2,0,1:T(4,128)S(1)} %convolution_bitcast_fusion.5), channel_id=1, replica_groups=mesh['branch'=2,'res'=16] {'res'}, dimensions={1}, use_global_device_ids=true | all-gather | bytes 156672 | tf_op jit(solution)/shard_map/all_gather | solution.py:189
  319.1 1.1 copy.331
  320.5 0.9 copy.274
  321.5 4.5 %all-to-all-start.4 = ((f32[96,6,128]{2,1,0:T(8,128)}), f32[96,6,128]{2,1,0:T(8,128)S(1)}, u32[]{:S(2)}, u32[]{:S(2)}) async-start(f32[96,6,128]{2,1,0:T(8,128)} %copy.274), calls=%async_computation.4 | async-start | bytes 786432 | tf_op jit(solution)/shard_map/all_to_all | solution.py:220
  327.1 11.0 %all-to-all-done.4 = f32[96,6,128]{2,1,0:T(8,128)S(1)} async-done(((f32[96,6,128]{2,1,0:T(8,128)}), f32[96,6,128]{2,1,0:T(8,128)S(1)}, u32[]{:S(2)}, u32[]{:S(2)}) %all-to-all-start.4) | async-done | bytes 294944 | tf_op jit(solution)/shard_map/all_to_all | solution.py:220
  339.3 8.0 %collective-permute-done.1 = f32[6,96,64]{2,1,0:T(8,128)S(1)} collective-permute-done((f32[6,96,64]{2,1,0:T(8,128)S(1)}, f32[6,96,64]{2,1,0:T(8,128)S(1)}, u32[]{:S(2)}, u32[]{:S(2)}) %collective-permute-start.1) | collective-permute-done | bytes 147488 | tf_op jit(solution)/shard_map/ppermute | solution.py:29
  (149 shorter events, 32.0 us)
Async XLA Ops:
  7.2 5.2 %copy-start = (f32[256,32]{0,1:T(8,128)S(1)}, f32[256,32]{0,1:T(8,128)}, u32[]{:S(2)}) copy-start(f32[256,32]{0,1:T(8,128)} %param.42) | copy-start | bytes 98308
  7.2 3.6 %copy-start.2 = (f32[128,6,256]{2,0,1:T(8,128)S(1)}, f32[128,6,256]{2,0,1:T(8,128)}, u32[]{:S(2)}) copy-start(f32[128,6,256]{2,0,1:T(8,128)} %param.34) | copy-start | bytes 2359300
  7.2 50.6 %all-gather.3.cloned.1.call-start = ((), (), s32[]{:S(2)}) async-start(), calls=%async_computation.5 | async-start | bytes 1671168 | tf_op jit(solution)/shard_map/all_gather | solution.py:152
  8.6 3.7 %copy-start.12 = (s32[128,6]{0,1:T(8,128)S(1)}, s32[128,6]{0,1:T(8,128)}, u32[]{:S(2)}) copy-start(s32[128,6]{0,1:T(8,128)} %param.36) | copy-start | bytes 9220
  10.8 12.7 %copy-start.17 = (u32[32]{0:T(128)S(1)}, u32[32]{0:T(128)}, u32[]{:S(2)}) copy-start(u32[32]{0:T(128)} %constant.198) | copy-start | bytes 388
  10.8 35.9 %copy-start.11 = (f32[256,32]{0,1:T(8,128)S(1)}, f32[256,32]{0,1:T(8,128)}, u32[]{:S(2)}) copy-start(f32[256,32]{0,1:T(8,128)} %param.41) | copy-start | bytes 98308
  12.4 45.4 %copy-start.1 = (f32[1024,128]{1,0:T(8,128)S(1)}, f32[1024,128]{1,0:T(8,128)}, u32[]{:S(2)}) copy-start(f32[1024,128]{1,0:T(8,128)} %param.43) | copy-start | bytes 1572868
  16.0 111.7 %all-to-all-start.1 = ((f32[16,8,6]{1,2,0:T(8,128)}), f32[16,8,6]{1,2,0:T(8,128)}, u32[]{:S(2)}, u32[]{:S(2)}) async-start(f32[16,8,6]{1,2,0:T(8,128)} %copy.256), calls=%async_computation.1 | async-start | bytes 131072 | tf_op jit(solution)/shard_map/all_to_all | solution.py:120
  23.4 102.8 %all-reduce.3.cloned.1.call-start = ((), (), s32[]{:S(2)}) async-start(), calls=%async_computation.6 | async-start | bytes 589824 | tf_op jit(solution)/shard_map/psum | solution.py:19
  57.8 36.9 %copy-start.16 = (s32[6]{0:T(128)S(1)}, s32[6]{0:T(128)}, u32[]{:S(2)}) copy-start(s32[6]{0:T(128)} %param.37) | copy-start | bytes 76
  57.8 68.4 %copy-start.3 = (f32[6,96,128]{2,1,0:T(8,128)S(1)}, f32[6,96,128]{2,1,0:T(8,128)}, u32[]{:S(2)}) copy-start(f32[6,96,128]{2,1,0:T(8,128)} %param.35) | copy-start | bytes 884740
  127.4 4.4 %copy-start.14 = (f32[128,4]{0,1:T(4,128)S(1)}, f32[128,4]{0,1:T(4,128)}, u32[]{:S(2)}) copy-start(f32[128,4]{0,1:T(4,128)} %param.45) | copy-start | bytes 6148
  127.7 37.9 %copy-start.7 = (f32[4,128,128]{2,1,0:T(8,128)S(1)}, f32[4,128,128]{2,1,0:T(8,128)}, u32[]{:S(2)}) copy-start(f32[4,128,128]{2,1,0:T(8,128)} %param.44) | copy-start | bytes 786436
  127.7 37.9 %copy-start.9 = (f32[128,128]{1,0:T(8,128)S(1)}, f32[128,128]{1,0:T(8,128)}, u32[]{:S(2)}) copy-start(f32[128,128]{1,0:T(8,128)} %param.46) | copy-start | bytes 196612
  127.7 39.6 %all-to-all-start = ((f32[128,6,256]{2,1,0:T(8,128)}), f32[128,6,256]{2,1,0:T(8,128)S(1)}, u32[]{:S(2)}, u32[]{:S(2)}) async-start(f32[128,6,256]{2,1,0:T(8,128)} %fusion.80), calls=%async_computation | async-start | bytes 2097152 | tf_op jit(solution)/shard_map/all_to_all | solution.py:119
  165.6 7.6 %copy-start.13 = (f32[128,8]{0,1:T(8,128)S(1)}, f32[128,8]{0,1:T(8,128)}, u32[]{:S(2)}) copy-start(f32[128,8]{0,1:T(8,128)} %param.40) | copy-start | bytes 12292
  167.3 118.3 %all-to-all-start.3 = ((f32[6,96,128]{2,0,1:T(8,128)}), f32[6,96,128]{2,0,1:T(8,128)}, u32[]{:S(2)}, u32[]{:S(2)}) async-start(f32[6,96,128]{2,0,1:T(8,128)} %fusion.85), calls=%async_computation.3 | async-start | bytes 786432 | tf_op jit(solution)/shard_map/all_to_all | solution.py:191
  231.1 1.5 copy-start.6
  242.0 39.2 %copy-start.8 = (f32[256,256]{1,0:T(8,128)S(1)}, f32[256,256]{1,0:T(8,128)}, u32[]{:S(2)}) copy-start(f32[256,256]{1,0:T(8,128)} %get-tuple-element.359) | copy-start | bytes 786436 | tf_op jit(solution)/shard_map/cond
  284.2 5.1 %copy-start.15 = (f32[128,4]{0,1:T(4,128)S(1)}, f32[128,4]{0,1:T(4,128)}, u32[]{:S(2)}) copy-start(f32[128,4]{0,1:T(4,128)} %param.48) | copy-start | bytes 6148
  285.6 34.6 %copy-start.10 = (f32[128,128]{1,0:T(8,128)S(1)}, f32[128,128]{1,0:T(8,128)}, u32[]{:S(2)}) copy-start(f32[128,128]{1,0:T(8,128)} %param.49) | copy-start | bytes 196612
  285.6 35.9 %all-to-all-start.2 = ((f32[8,96,256]{2,0,1:T(8,128)}), f32[8,96,256]{2,0,1:T(8,128)S(1)}, u32[]{:S(2)}, u32[]{:S(2)}) async-start(f32[8,96,256]{2,0,1:T(8,128)} %copy.260), calls=%async_computation.2 | async-start | bytes 1572864 | tf_op jit(solution)/shard_map/all_to_all | solution.py:147
  321.5 16.6 %all-to-all-start.4 = ((f32[96,6,128]{2,1,0:T(8,128)}), f32[96,6,128]{2,1,0:T(8,128)S(1)}, u32[]{:S(2)}, u32[]{:S(2)}) async-start(f32[96,6,128]{2,1,0:T(8,128)} %copy.274), calls=%async_computation.4 | async-start | bytes 786432 | tf_op jit(solution)/shard_map/all_to_all | solution.py:220
  326.1 0.9 copy-start.4
  327.0 11.5 %copy-start.5 = (f32[128,6,256]{2,0,1:T(8,128)S(1)}, f32[128,6,256]{2,0,1:T(8,128)}, u32[]{:S(2)}) copy-start(f32[128,6,256]{2,0,1:T(8,128)} %copy-done.4) | copy-start | bytes 2359300
  327.0 11.5 %collective-permute-start = (f32[64,6,256]{2,0,1:T(8,128)S(1)}, f32[64,6,256]{2,0,1:T(8,128)S(1)}, u32[]{:S(2)}, u32[]{:S(2)}) collective-permute-start(f32[64,6,256]{2,0,1:T(8,128)S(1)} %slice.53), channel_id=1, source_target_pairs={{0,16},{16,0},{1,17},{17,1},{2,18},{18,2},{3,19},{19,3},{4,20},{20... | collective-permute-start | bytes 1179656 | tf_op jit(solution)/shard_map/ppermute | solution.py:29
  338.2 9.1 %collective-permute-start.1 = (f32[6,96,64]{2,1,0:T(8,128)S(1)}, f32[6,96,64]{2,1,0:T(8,128)S(1)}, u32[]{:S(2)}, u32[]{:S(2)}) collective-permute-start(f32[6,96,64]{2,1,0:T(8,128)S(1)} %bitcast.264), channel_id=1, source_target_pairs={{0,16},{16,0},{1,17},{17,1},{2,18},{18,2},{3,19},{19,3},{4,20},{20... | collective-permute-start | bytes 442376 | tf_op jit(solution)/shard_map/ppermute | solution.py:29
Sparse Core Ops, SparseCore 0:
  15.4 42.3 all-gather.2
  94.8 21.5 all-reduce.2
where the time goes:
time: 357 us; the launch traced here: 355 us
  blocking collectives  171 us (48%)
  matrix products  59.8 us (17%)
  local copies, waits for them, and re-layouts  30.1 us (8%)
  waiting for transfers between devices  28.2 us (8%)
  starting transfers between devices  25.5 us (7%)
  other arithmetic  24.2 us (7%)
  between operations  15.1 us (4%)
    psum x1, blocking collectives, spread(): return lax.psum(jnp.where(mine, value, jnp.zeros_like(value)), axis)  33.9 us
    all_gather x1, blocking collectives, per_device(): lax.all_gather(start_rows, 'res', axis=1, tiled=True)  33.2 us
    unnamed x1, blocking collectives  31.4 us
    all_gather x1, blocking collectives, per_device(): end_full = lax.all_gather(end_rows, 'res', axis=1, tiled=True)  28.1 us
    dot_general x13, matrix products, linear_project(): jnp.dot(values, weight, precision=highest, preferred_element_type=jnp.flo...  26.3 us
    all_gather x1, blocking collectives, per_device(): row_bias = lax.all_gather(own_rows, 'res', axis=1, tiled=True)  22.8 us
    all_gather x1, blocking collectives, per_device(): lax.all_gather(mask_rows, 'res', axis=0, tiled=True)  21.9 us
    dot_general x6, matrix products, outer_one_row(): jnp.einsum('cs,jes->jce', row_left, right_all, precision=highest)  19.8 us
  transfers between devices with their start and end apart: 9, of which 4 were waited for; matrix products, arithmetic and copies ran while one was open for 29% of the time, Pallas kernels for 0%

commit v1 on v0

v1 whole, which is shorter than its diff:
```python
import functools
import math

import jax
import jax.numpy as jnp
from jax import lax
from jax.experimental import pallas as pl
from jax.experimental.pallas import tpu as pltpu
from jax.sharding import PartitionSpec as P

epsilon = 1e-05
masked_score = -1000000000.0
EVERYONE = ("res", "branch")

NN = (((1,), (0,)), ((), ()))
NT = (((1,), (1,)), ((), ()))


def layer_normalize(values):
    centred = values - jnp.mean(values, axis=-1, keepdims=True)
    variance = jnp.mean(centred * centred, axis=-1, keepdims=True)
    return centred * lax.rsqrt(variance + epsilon)


def split(values):
    high = values.astype(jnp.bfloat16)
    return high, (values - high.astype(jnp.float32)).astype(jnp.bfloat16)


def dot3(a, b, dims=NN):
    (ah, al), (bh, bl) = a, b

    def one(x, y):
        return lax.dot_general(x, y, dims, preferred_element_type=jnp.float32)

    return one(ah, bh) + (one(ah, bl) + one(al, bh))


def attention_kernel(heads, x_ref, bias_ref, live_ref, proj_ref, out_w_ref, *rest):
    next_w_ref, o_ref, next_ref = rest if len(rest) == 3 else (None, rest[0], None)
    x = x_ref[0]
    channels = x.shape[1]
    width = channels // heads
    normed = split(layer_normalize(x))
    q, k, v, g = (dot3(normed, split(proj_ref[p])) for p in range(4))
    q = q * (1.0 / math.sqrt(width))
    keys = split(k)
    owner = lax.broadcasted_iota(jnp.int32, (1, channels), 1) // width
    live = live_ref[0] > 0.5
    mixture = None
    for h in range(heads):
        mine = owner == h
        scores = dot3(split(jnp.where(mine, q, 0.0)), keys, NT) + bias_ref[h]
        scores = jnp.where(live, scores, masked_score)
        weights = jnp.exp(scores - jnp.max(scores, axis=-1, keepdims=True))
        weights = weights / jnp.sum(weights, axis=-1, keepdims=True)
        term = dot3(split(weights), split(jnp.where(mine, v, 0.0)))
        mixture = term if mixture is None else mixture + term
    gated = jax.nn.sigmoid(g) * mixture
    result = x + dot3(split(gated), split(out_w_ref[...]))
    o_ref[0] = result
    if next_ref is not None:
        next_ref[0] = dot3(split(next_w_ref[...]), split(layer_normalize(result)), NT)


def attention(x, bias, live, proj, out_w, heads, next_w=None):
    lines, residues, channels = x.shape

    def whole(a):
        return pl.BlockSpec(a.shape, lambda i: (0,) * a.ndim)

    line = pl.BlockSpec((1, residues, channels), lambda i: (i, 0, 0))
    args = [x, bias, live, proj, out_w]
    in_specs = [
        line,
        whole(bias),
        pl.BlockSpec((1, 1, residues), lambda i: (i, 0, 0)),
        whole(proj),
        whole(out_w),
    ]
    out_shape = [jax.ShapeDtypeStruct(x.shape, jnp.float32)]
    out_specs = [line]
    if next_w is not None:
        args.append(next_w)
        in_specs.append(whole(next_w))
        out_shape.append(
            jax.ShapeDtypeStruct((lines, next_w.shape[0], residues), jnp.float32)
        )
        out_specs.append(
            pl.BlockSpec((1, next_w.shape[0], residues), lambda i: (i, 0, 0))
        )
    return pl.pallas_call(
        functools.partial(attention_kernel, heads),
        grid=(lines,),
        in_specs=in_specs,
        out_specs=out_specs,
        out_shape=out_shape,
    )(*args)


def outer_kernel(left_ref, right_ref, weight_ref, o_ref):
    rows, factors, sequences = left_ref.shape
    shares, half, padded, _ = right_ref.shape
    columns = shares * padded
    left = split(left_ref[...].reshape(rows * factors, sequences))
    weight = split(weight_ref[...])
    products = []
    for e in range(half):
        right = split(right_ref[:, e].reshape(columns, sequences))
        products.append(dot3(left, right, NT))
    for i in range(rows):
        block = jnp.concatenate(
            [one[i * factors : (i + 1) * factors] for one in products], axis=0
        )
        o_ref[i] = jnp.transpose(dot3(weight, split(block)))


def outer_product(left, right, weight):
    rows = left.shape[0]
    columns = right.shape[0] * right.shape[2]
    return pl.pallas_call(
        outer_kernel,
        out_shape=jax.ShapeDtypeStruct((rows, columns, weight.shape[0]), jnp.float32),
    )(left, right, weight)


def project(a, b, form):
    return jnp.einsum(form, a, b, precision=lax.Precision.HIGH)


def gather(block, axes, count):
    copies = jnp.broadcast_to(block[None], (count,) + block.shape)
    return lax.all_to_all(copies, axes, 0, 0)


def per_device(
    msa,
    pair,
    msa_mask,
    residue_mask,
    row_proj,
    row_out,
    row_bias_w,
    first_w,
    other_w,
    outer_w,
    start_proj,
    start_bias_w,
    start_out,
    end_proj,
    end_bias_w,
    end_out,
):
    b = lax.axis_index("branch")
    branches = lax.axis_size("branch")
    shares = lax.axis_size("res")
    everyone = branches * shares
    sequences, local, features = msa.shape
    residues, width = pair.shape[1:]
    factors = first_w.shape[1]
    half = factors // branches
    mine = local // branches
    per_seq = sequences // everyone
    padded = -(-local // 8) * 8

    depth = jnp.sum(msa_mask, axis=0).astype(jnp.float32)
    bias_rows = project(layer_normalize(pair), row_bias_w, "ijc,ch->ihj")
    bias_pack = jnp.concatenate(
        [bias_rows, jnp.broadcast_to(depth[:, None, None], (local, 1, residues))], axis=1
    )

    normed = layer_normalize(msa)
    my_other = lax.dynamic_slice_in_dim(other_w, b * half, half, axis=1)
    mask = jnp.transpose(msa_mask).astype(jnp.float32)
    left = project(normed, first_w, "sia,ac->ics") * mask[:, None, :]
    right = project(normed, my_other, "sja,ae->ejs") * mask[None]
    right = jnp.pad(right, ((0, 0), (0, padded - local), (0, 0)))
    right_all = gather(right, "res", shares)

    bias_all = gather(bias_pack, "res", shares).reshape(residues, -1, residues)
    row_bias = jnp.transpose(bias_all[:, :-1], (1, 0, 2))
    depth_all = bias_all[:, -1, 0]

    my_msa = lax.dynamic_slice_in_dim(msa, b * (sequences // branches), sequences // branches, axis=0)
    seq_msa = lax.all_to_all(my_msa, "res", split_axis=0, concat_axis=1, tiled=True)

    weight = outer_w.reshape(factors, factors, width)
    weight = lax.dynamic_slice_in_dim(weight, b * half, half, axis=1)
    weight = jnp.transpose(weight, (2, 1, 0)).reshape(width, half * factors)
    partial = outer_product(left, right_all, weight)
    partial = partial.reshape(branches, mine, shares, padded, width)[:, :, :, :local]
    partial = partial.reshape(branches, mine, residues, width)
    update = jnp.sum(lax.all_to_all(partial, "branch", 0, 0), axis=0)
    my_depth = lax.dynamic_slice_in_dim(depth, b * mine, mine)
    overlap = jnp.minimum(my_depth[:, None], depth_all[None])
    my_pair = lax.dynamic_slice_in_dim(pair, b * mine, mine)
    pair_one = my_pair + update / jnp.maximum(overlap, 1.0)[:, :, None]

    start_rows = project(layer_normalize(pair_one), start_bias_w, "ijc,ch->ihj")
    start_all = gather(start_rows, EVERYONE, everyone)
    heads_z = start_bias_w.shape[1]
    start_score = jnp.transpose(start_all.reshape(residues, heads_z, residues), (1, 0, 2))
    live = jnp.broadcast_to((depth_all > 0.5).astype(jnp.float32), (mine, 1, residues))
    next_w = jnp.pad(jnp.transpose(end_bias_w), ((0, -heads_z % 8), (0, 0)))
    pair_two, end_rows = attention(
        pair_one, start_score, live, start_proj, start_out, heads_z, next_w
    )
    end_all = gather(end_rows[:, :heads_z], EVERYONE, everyone)
    end_score = jnp.transpose(end_all.reshape(residues, heads_z, residues), (1, 2, 0))

    columns = lax.all_to_all(
        pair_two.reshape(mine, everyone, mine, width), EVERYONE, 1, 0
    )
    columns = jnp.transpose(columns.reshape(residues, mine, width), (1, 0, 2))

    start_of_seq = (b * shares + lax.axis_index("res")) * per_seq
    present = (
        start_of_seq + jnp.arange(per_seq)[:, None, None] < depth_all[None, None, :]
    ).astype(jnp.float32)
    (seq_result,) = attention(
        seq_msa, row_bias, present, row_proj, row_out, row_bias_w.shape[1]
    )
    msa_result = lax.all_to_all(seq_result, "res", split_axis=1, concat_axis=0, tiled=True)

    (end_result,) = attention(columns, end_score, live, end_proj, end_out, heads_z)
    tiles = end_result.reshape(mine, shares, local, branches, width // branches)
    tiles = jnp.transpose(tiles, (1, 3, 2, 0, 4)).reshape(
        everyone, local, mine, width // branches
    )
    pair_result = lax.all_to_all(tiles, EVERYONE, 0, 0)
    pair_result = jnp.transpose(pair_result, (1, 0, 2, 3)).reshape(
        local, residues, width // branches
    )
    return msa_result, pair_result


def solution(mesh):
    in_specs = (
        P(None, "res", None),
        P("res", None, None),
        P(None, "res"),
        P("res"),
    ) + (P(),) * 12
    out_specs = (P("branch", "res", None), P("res", None, "branch"))
    return jax.shard_map(
        per_device, mesh=mesh, in_specs=in_specs, out_specs=out_specs, check_vma=False
    )
```

time: 357 us -> 177 us (0.50)
  blocking collectives: 171 us -> 0 us
  matrix products: 59.8 us -> 2.63 us
  waiting for transfers between devices: 28.2 us -> 69.3 us
  Pallas kernels: 0 us -> 31.5 us
  other arithmetic: 24.2 us -> 4.97 us
  starting transfers between devices: 25.5 us -> 40.2 us
  between operations: 15.1 us -> 1.08 us
    all_gather x4 -> x0, blocking collectives: 106 us -> none  [the longest x1 33.2 us: per_device(): lax.all_gather(start_rows, 'res', axis=1, tiled=True)]
    all_to_all x5 -> x9, waiting for transfers between devices: 11.1 us -> 69.3 us  [the longest x4 40.8 us: gather(): return lax.all_to_all(copies, axes, 0, 0)]
    dot_general x43 -> x4, matrix products: 59.8 us -> 2.63 us  [project(): return jnp.einsum(form, a, b, precision=lax.Precision.HIGH)]
    psum x1 -> x0, blocking collectives: 33.9 us -> none  [spread(): return lax.psum(jnp.where(mine, value, jnp.zeros_like(value)), axis)]
    pallas_call x0 -> x4, Pallas kernels: none -> 31.5 us  [the longest x3 27.5 us: attention(): pl.pallas_call(functools.partial(attention_kernel, heads), grid=(lines,),...]
    unnamed x1 -> x0, blocking collectives: 31.4 us -> none
    all_to_all x5 -> x9, starting transfers between devices: 25.3 us -> 40.2 us  [the longest x4 19.9 us: gather(): return lax.all_to_all(copies, axes, 0, 0)]
    dynamic_slice x16 -> x2, local copies, waits for them, and re-layouts: 14.8 us -> 0.11 us  [the longest x1 0.07 us: per_device(): my_depth = lax.dynamic_slice_in_dim(depth, b * mine, mine)]
  transfers between devices with their start and end apart: 9 -> 9, of which waited for: 4 -> 8; matrix products, arithmetic and copies ran while one was open for 29% -> 11% of each run, Pallas kernels for 0% -> 16%
where the time goes in v1:
time: 177 us; the launch traced here: 176 us
  waiting for transfers between devices  69.3 us (39%)
  starting transfers between devices  40.2 us (23%)
  Pallas kernels  31.5 us (18%)
  local copies, waits for them, and re-layouts  26.6 us (15%)
  other arithmetic  4.97 us (3%)
  matrix products  2.63 us (1%)
    all_to_all x4, waiting for transfers between devices, gather(): return lax.all_to_all(copies, axes, 0, 0)  40.8 us
    pallas_call x3, Pallas kernels, attention(): pl.pallas_call(functools.partial(attention_kernel, heads), grid=(lines,),...  27.5 us
    all_to_all x4, starting transfers between devices, gather(): return lax.all_to_all(copies, axes, 0, 0)  19.9 us
    all_to_all x1, waiting for transfers between devices, per_device(): lax.all_to_all(pair_two.reshape(mine, everyone, mine, width), EVERYONE, 1...  8.82 us
    all_to_all x1, waiting for transfers between devices, per_device(): pair_result = lax.all_to_all(tiles, EVERYONE, 0, 0)  7.94 us
    unnamed x28, local copies, waits for them, and re-layouts  7.02 us
    all_to_all x1, waiting for transfers between devices, per_device(): update = jnp.sum(lax.all_to_all(partial, 'branch', 0, 0), axis=0)  6.58 us
    all_to_all x1, starting transfers between devices, per_device(): lax.all_to_all(seq_result, 'res', split_axis=1, concat_axis=0, tiled=True)  5.92 us
  transfers between devices with their start and end apart: 9, of which 8 were waited for; matrix products, arithmetic and copies ran while one was open for 11% of the time, Pallas kernels for 16%

profile of v1, /device:TPU:0, one launch (start us, length us, event | category | flops | bytes accessed | tf_op | source)
XLA Modules:
  0.0 176.1 jit_solution(8457147339185652804)
XLA Ops:
  0.7 0.9 convert_bitcast_fusion
  1.6 1.1 reduce_sum.72
  2.7 0.3 multiply_reduce_fusion.1
  3.0 0.7 copy-done.7
  3.7 0.5 convolution_bitcast_fusion.2
  4.3 0.8 broadcast_in_dim.13
  5.2 7.4 %all-to-all-start.1 = ((f32[16,6,9,96]{3,1,2,0:T(8,128)}), f32[16,6,9,96]{3,1,2,0:T(8,128)S(1)}, u32[]{:S(2)}, u32[]{:S(2)}) async-start(f32[16,6,9,96]{3,1,2,0:T(8,128)} %broadcast_in_dim.13), calls=%async_computation.1 | async-start | bytes 1179648 | tf_op jit(solution)/shard_map/all_to_all | solution.py:133
  12.8 0.3 multiply_reduce_fusion
  13.1 0.4 copy-done.6
  13.6 0.6 fusion.1
  14.2 13.8 %all-to-all-done.1 = f32[16,6,9,96]{3,1,2,0:T(8,128)S(1)} async-done(((f32[16,6,9,96]{3,1,2,0:T(8,128)}), f32[16,6,9,96]{3,1,2,0:T(8,128)S(1)}, u32[]{:S(2)}, u32[]{:S(2)}) %all-to-all-start.1) | async-done | bytes 331808 | tf_op jit(solution)/shard_map/all_to_all | solution.py:133
  28.0 1.1 broadcast_in_dim.14
  29.0 4.5 %all-to-all-start.3 = ((f32[16,16,8,128]{3,2,1,0:T(8,128)}), f32[16,16,8,128]{3,2,1,0:T(8,128)S(1)}, u32[]{:S(2)}, u32[]{:S(2)}) async-start(f32[16,16,8,128]{3,2,1,0:T(8,128)} %broadcast_in_dim.14), calls=%async_computation.3 | async-start | bytes 2097152 | tf_op jit(solution)/shard_map/all_to_all | solution.py:133
  33.7 0.8 copy.104.weight_ref
  34.6 1.3 fusion.left_ref
  35.8 0.9 copy.97
  36.7 1.1 reshape.180
  37.9 18.5 %all-to-all-done.3.right_ref = f32[16,16,8,128]{3,2,1,0:T(8,128)S(1)} async-done(((f32[16,16,8,128]{3,2,1,0:T(8,128)}), f32[16,16,8,128]{3,2,1,0:T(8,128)S(1)}, u32[]{:S(2)}, u32[]{:S(2)}) %all-to-all-start.3) | async-done | bytes 1048608 | tf_op jit(solution)/shard_map/all_to_all | solution.py:133
  56.4 1.0 copy-done.2
  57.4 4.0 %shard_map.159 = f32[6,128,128]{2,1,0:T(8,128)} custom-call(f32[6,32,128]{2,1,0:T(8,128)} %fusion.left_ref, f32[16,16,8,128]{3,2,1,0:T(8,128)} %copy-done.2, f32[128,512]{1,0:T(8,128)} %copy.104.weight_ref), custom_call_target="tpu_custom_call" | custom-call | tf_op jit(solution)/shard_map/pallas_call | solution.py:121
  61.3 1.2 copy.117
  62.5 0.7 copy.106
  63.3 3.4 %all-to-all-start.4 = ((f32[2,3,96,128]{3,2,1,0:T(8,128)}), f32[2,3,96,128]{3,2,1,0:T(8,128)S(1)}, u32[]{:S(2)}, u32[]{:S(2)}) async-start(f32[2,3,96,128]{3,2,1,0:T(8,128)} %copy.106), calls=%async_computation.4 | async-start | bytes 589824 | tf_op jit(solution)/shard_map/all_to_all | solution.py:193
  66.8 6.6 %all-to-all-done.4 = f32[2,3,96,128]{3,2,1,0:T(8,128)S(1)} async-done(((f32[2,3,96,128]{3,2,1,0:T(8,128)}), f32[2,3,96,128]{3,2,1,0:T(8,128)S(1)}, u32[]{:S(2)}, u32[]{:S(2)}) %all-to-all-start.4) | async-done | bytes 294944 | tf_op jit(solution)/shard_map/all_to_all | solution.py:193
  73.4 0.2 fusion.24
  73.7 0.2 multiply_reduce_fusion.2
  73.9 0.7 copy-done.9
  74.6 0.3 convolution_bitcast_fusion.3
  74.9 0.8 broadcast_in_dim.15
  75.6 5.5 %all-to-all-start.5 = ((f32[32,3,4,96]{3,2,1,0:T(4,128)}), f32[32,3,4,96]{3,2,1,0:T(4,128)S(1)}, u32[]{:S(2)}, u32[]{:S(2)}) async-start(f32[32,3,4,96]{3,2,1,0:T(4,128)} %broadcast_in_dim.15), calls=%async_computation.5 | async-start | bytes 393216 | tf_op jit(solution)/shard_map/all_to_all | solution.py:133
  81.1 1.0 copy.116
  82.2 8.6 %all-to-all-done.5 = f32[32,3,4,96]{3,2,1,0:T(4,128)S(1)} async-done(((f32[32,3,4,96]{3,2,1,0:T(4,128)}), f32[32,3,4,96]{3,2,1,0:T(4,128)S(1)}, u32[]{:S(2)}, u32[]{:S(2)}) %all-to-all-start.5) | async-done | bytes 147488 | tf_op jit(solution)/shard_map/all_to_all | solution.py:133
  90.7 3.7 %all-to-all-start = ((f32[64,6,256]{2,1,0:T(8,128)}), f32[64,6,256]{2,1,0:T(8,128)S(1)}, u32[]{:S(2)}, u32[]{:S(2)}) async-start(f32[64,6,256]{2,1,0:T(8,128)} %copy.116), calls=%async_computation | async-start | bytes 1048576 | tf_op jit(solution)/shard_map/all_to_all | solution.py:185
  94.4 0.6 pad.9.rest_0_
  95.1 0.7 copy.121
  95.7 0.6 broadcast_in_dim.16.live_ref
  96.3 7.2 %shard_map.160 = (f32[3,96,128]{2,1,0:T(8,128)}, f32[3,8,96]{2,1,0:T(8,128)}) custom-call(f32[3,96,128]{2,1,0:T(8,128)} %copy-done.4, f32[4,96,96]{2,1,0:T(8,128)} %bitcast.77, f32[3,1,96]{2,1,0:T(1,128)} %broadcast_in_dim.16.live_ref, f32[4,128,128]{2,1,0:T(8,128)} %proj_ref.4, f32[128,128]{1,0:T(8,128)} %out_w_ref.4, f32[8,128]{1,0:T(8,128)} %pad.9.rest_0_), custom_call_target="tpu_custom_call" | custom-call | tf_op jit(solution)/shard_map/pallas_call | solution.py:92
  103.6 1.0 broadcast_in_dim_reshape.3
  104.5 0.8 copy.108
  105.4 3.3 %all-to-all-done = f32[64,6,256]{2,1,0:T(8,128)S(1)} async-done(((f32[64,6,256]{2,1,0:T(8,128)}), f32[64,6,256]{2,1,0:T(8,128)S(1)}, u32[]{:S(2)}, u32[]{:S(2)}) %all-to-all-start) | async-done | bytes 393248 | tf_op jit(solution)/shard_map/all_to_all | solution.py:185
  108.7 3.1 %all-to-all-start.6 = ((f32[1,3,32,3,128]{4,0,3,1,2:T(1,128)}), f32[1,3,32,3,128]{4,0,3,1,2:T(1,128)S(1)}, u32[]{:S(2)}, u32[]{:S(2)}) async-start(f32[1,3,32,3,128]{4,0,3,1,2:T(1,128)} %copy.108), calls=%async_computation.6 | async-start | bytes 294912 | tf_op jit(solution)/shard_map/all_to_all | solution.py:211
  111.8 8.8 %all-to-all-done.6 = f32[1,3,32,3,128]{4,0,3,1,2:T(1,128)S(1)} async-done(((f32[1,3,32,3,128]{4,0,3,1,2:T(1,128)}), f32[1,3,32,3,128]{4,0,3,1,2:T(1,128)S(1)}, u32[]{:S(2)}, u32[]{:S(2)}) %all-to-all-start.6) | async-done | bytes 147488 | tf_op jit(solution)/shard_map/all_to_all | solution.py:211
  120.6 0.7 broadcast_in_dim.17
  121.3 2.6 %all-to-all-start.7 = ((f32[32,3,4,96]{3,2,1,0:T(4,128)}), f32[32,3,4,96]{3,2,1,0:T(4,128)S(1)}, u32[]{:S(2)}, u32[]{:S(2)}) async-start(f32[32,3,4,96]{3,2,1,0:T(4,128)} %broadcast_in_dim.17), calls=%async_computation.7 | async-start | bytes 393216 | tf_op jit(solution)/shard_map/all_to_all | solution.py:133
  124.0 0.6 compare_convert_fusion.live_ref
  124.6 0.8 slice_bitcast_fusion.bias_ref
  125.5 0.8 copy.99.x_ref
  126.3 14.0 %shard_map.158 = f32[4,96,256]{2,1,0:T(8,128)} custom-call(f32[4,96,256]{2,1,0:T(8,128)} %copy.99.x_ref, f32[8,96,96]{2,1,0:T(8,128)} %slice_bitcast_fusion.bias_ref, f32[4,1,96]{2,1,0:T(1,128)} %compare_convert_fusion.live_ref, f32[4,256,256]{2,1,0:T(8,128)} %proj_ref.3, f32[256,256]{1,0:T(8,128)} %out_w_ref.3), custom_call_target="tpu_custom_call" | custom-call | tf_op jit(solution)/shard_map/pallas_call | solution.py:92
  140.3 2.0 %copy.100 = f32[4,96,256]{2,0,1:T(4,128)} copy(f32[4,96,256]{2,1,0:T(8,128)} %shard_map.158) | data formatting | bytes 786432 | tf_op jit(solution)/shard_map/pallas_call | solution.py:92
  142.3 5.9 %all-to-all-start.2 = ((f32[4,96,256]{2,0,1:T(4,128)}), f32[4,96,256]{2,0,1:T(4,128)S(1)}, u32[]{:S(2)}, u32[]{:S(2)}) async-start(f32[4,96,256]{2,0,1:T(4,128)} %copy.100), calls=%async_computation.2 | async-start | bytes 786432 | tf_op jit(solution)/shard_map/all_to_all | solution.py:223
  148.4 0.7 reshape_squeeze.3
  149.1 0.8 copy.111
  149.9 6.3 %shard_map.161 = f32[3,96,128]{2,1,0:T(8,128)} custom-call(f32[3,96,128]{2,1,0:T(8,128)} %bitcast.80, f32[4,96,96]{2,1,0:T(8,128)} %bitcast.78, f32[3,1,96]{2,1,0:T(1,128)} %broadcast_in_dim.16.live_ref, f32[4,128,128]{2,1,0:T(8,128)} %proj_ref.5, f32[128,128]{1,0:T(8,128)} %out_w_ref.5), custom_call_target="tpu_custom_call" | custom-call | tf_op jit(solution)/shard_map/pallas_call | solution.py:92
  156.2 1.1 reshape.187
  157.4 0.2 copy.113
  157.6 1.0 reshape.195
  158.6 1.8 %all-to-all-done.2 = f32[4,96,256]{2,0,1:T(4,128)S(1)} async-done(((f32[4,96,256]{2,0,1:T(4,128)}), f32[4,96,256]{2,0,1:T(4,128)S(1)}, u32[]{:S(2)}, u32[]{:S(2)}) %all-to-all-start.2) | async-done | bytes 393248 | tf_op jit(solution)/shard_map/all_to_all | solution.py:223
  160.4 4.1 %all-to-all-start.8 = ((f32[32,1,1152]{2,1,0:T(1,128)}), f32[32,1,1152]{2,1,0:T(1,128)S(1)}, u32[]{:S(2)}, u32[]{:S(2)}) async-start(f32[32,1,1152]{2,1,0:T(1,128)} %reshape.195), calls=%async_computation.8 | async-start | bytes 294912 | tf_op jit(solution)/shard_map/all_to_all | solution.py:230
  164.6 0.9 all_to_all.63
  165.4 7.9 %all-to-all-done.8 = f32[32,1,1152]{2,1,0:T(1,128)S(1)} async-done(((f32[32,1,1152]{2,1,0:T(1,128)}), f32[32,1,1152]{2,1,0:T(1,128)S(1)}, u32[]{:S(2)}, u32[]{:S(2)}) %all-to-all-start.8) | async-done | bytes 147488 | tf_op jit(solution)/shard_map/all_to_all | solution.py:230
  173.4 0.5 broadcast.144
  173.9 1.0 reduce.2
  174.9 0.2 reshape.196
  175.3 0.8 copy.115
  (50 shorter events, 1.6 us)
Async XLA Ops:
  0.6 32.9 %copy-start = (f32[1024,128]{1,0:T(8,128)S(1)}, f32[1024,128]{1,0:T(8,128)}, u32[]{:S(2)}) copy-start(f32[1024,128]{1,0:T(8,128)} %param.24) | copy-start | bytes 1572868
  0.6 2.1 %copy-start.3 = (f32[6,96,128]{2,1,0:T(8,128)S(1)}, f32[6,96,128]{2,1,0:T(8,128)}, u32[]{:S(2)}) copy-start(f32[6,96,128]{2,1,0:T(8,128)} %param.17) | copy-start | bytes 884740
  3.0 0.7 copy-start.7
  4.3 8.3 %copy-start.1 = (f32[128,6,256]{2,0,1:T(8,128)S(1)}, f32[128,6,256]{2,0,1:T(8,128)}, u32[]{:S(2)}) copy-start(f32[128,6,256]{2,0,1:T(8,128)} %param.16) | copy-start | bytes 2359300
  5.2 22.8 %all-to-all-start.1 = ((f32[16,6,9,96]{3,1,2,0:T(8,128)}), f32[16,6,9,96]{3,1,2,0:T(8,128)S(1)}, u32[]{:S(2)}, u32[]{:S(2)}) async-start(f32[16,6,9,96]{3,1,2,0:T(8,128)} %broadcast_in_dim.13), calls=%async_computation.1 | async-start | bytes 1179648 | tf_op jit(solution)/shard_map/all_to_all | solution.py:133
  12.8 0.8 copy-start.6
  29.0 27.4 %all-to-all-start.3 = ((f32[16,16,8,128]{3,2,1,0:T(8,128)}), f32[16,16,8,128]{3,2,1,0:T(8,128)S(1)}, u32[]{:S(2)}, u32[]{:S(2)}) async-start(f32[16,16,8,128]{3,2,1,0:T(8,128)} %broadcast_in_dim.14), calls=%async_computation.3 | async-start | bytes 2097152 | tf_op jit(solution)/shard_map/all_to_all | solution.py:133
  33.6 0.9 copy-start.5
  56.4 1.0 copy-start.2
  63.3 10.1 %all-to-all-start.4 = ((f32[2,3,96,128]{3,2,1,0:T(8,128)}), f32[2,3,96,128]{3,2,1,0:T(8,128)S(1)}, u32[]{:S(2)}, u32[]{:S(2)}) async-start(f32[2,3,96,128]{3,2,1,0:T(8,128)} %copy.106), calls=%async_computation.4 | async-start | bytes 589824 | tf_op jit(solution)/shard_map/all_to_all | solution.py:193
  73.6 1.2 copy-start.4
  73.9 0.7 copy-start.9
  75.6 15.1 %all-to-all-start.5 = ((f32[32,3,4,96]{3,2,1,0:T(4,128)}), f32[32,3,4,96]{3,2,1,0:T(4,128)S(1)}, u32[]{:S(2)}, u32[]{:S(2)}) async-start(f32[32,3,4,96]{3,2,1,0:T(4,128)} %broadcast_in_dim.15), calls=%async_computation.5 | async-start | bytes 393216 | tf_op jit(solution)/shard_map/all_to_all | solution.py:133
  90.7 3.7 %copy-start.10 = (f32[128,4]{0,1:T(4,128)S(1)}, f32[128,4]{0,1:T(4,128)}, u32[]{:S(2)}) copy-start(f32[128,4]{0,1:T(4,128)} %param.29) | copy-start | bytes 6148
  90.7 17.9 %all-to-all-start = ((f32[64,6,256]{2,1,0:T(8,128)}), f32[64,6,256]{2,1,0:T(8,128)S(1)}, u32[]{:S(2)}, u32[]{:S(2)}) async-start(f32[64,6,256]{2,1,0:T(8,128)} %copy.116), calls=%async_computation | async-start | bytes 1048576 | tf_op jit(solution)/shard_map/all_to_all | solution.py:185
  108.7 3.1 %copy-start.8 = (f32[3,8,96]{2,1,0:T(8,128)S(1)}, f32[3,8,96]{2,1,0:T(8,128)}, u32[]{:S(2)}) copy-start(f32[3,8,96]{2,1,0:T(8,128)} %get-tuple-element.5) | copy-start | bytes 27652
  108.7 11.9 %all-to-all-start.6 = ((f32[1,3,32,3,128]{4,0,3,1,2:T(1,128)}), f32[1,3,32,3,128]{4,0,3,1,2:T(1,128)S(1)}, u32[]{:S(2)}, u32[]{:S(2)}) async-start(f32[1,3,32,3,128]{4,0,3,1,2:T(1,128)} %copy.108), calls=%async_computation.6 | async-start | bytes 294912 | tf_op jit(solution)/shard_map/all_to_all | solution.py:211
  121.3 21.0 %all-to-all-start.7 = ((f32[32,3,4,96]{3,2,1,0:T(4,128)}), f32[32,3,4,96]{3,2,1,0:T(4,128)S(1)}, u32[]{:S(2)}, u32[]{:S(2)}) async-start(f32[32,3,4,96]{3,2,1,0:T(4,128)} %broadcast_in_dim.17), calls=%async_computation.7 | async-start | bytes 393216 | tf_op jit(solution)/shard_map/all_to_all | solution.py:133
  142.3 18.1 %all-to-all-start.2 = ((f32[4,96,256]{2,0,1:T(4,128)}), f32[4,96,256]{2,0,1:T(4,128)S(1)}, u32[]{:S(2)}, u32[]{:S(2)}) async-start(f32[4,96,256]{2,0,1:T(4,128)} %copy.100), calls=%async_computation.2 | async-start | bytes 786432 | tf_op jit(solution)/shard_map/all_to_all | solution.py:223
  160.4 13.0 %all-to-all-start.8 = ((f32[32,1,1152]{2,1,0:T(1,128)}), f32[32,1,1152]{2,1,0:T(1,128)S(1)}, u32[]{:S(2)}, u32[]{:S(2)}) async-start(f32[32,1,1152]{2,1,0:T(1,128)} %reshape.195), calls=%async_computation.8 | async-start | bytes 294912 | tf_op jit(solution)/shard_map/all_to_all | solution.py:230

commit v2 on v1

--- a/solution.py
+++ b/solution.py
@@ -131,6 +131,501 @@
 def gather(block, axes, count):
     copies = jnp.broadcast_to(block[None], (count,) + block.shape)
     return lax.all_to_all(copies, axes, 0, 0)
+
+
+MESH = pl.DeviceIdType.MESH
+
+
+def rows_attention(x, bias_of, mask_of, proj, out_w, heads):
+    channels = x.shape[1]
+    width = channels // heads
+    normed = split(layer_normalize(x))
+    q, k, v, g = (dot3(normed, split(proj[p])) for p in range(4))
+    q = q * (1.0 / math.sqrt(width))
+    keys = split(k)
+    owner = lax.broadcasted_iota(jnp.int32, (1, channels), 1) // width
+    mixture = None
+    for h in range(heads):
+        mine = owner == h
+        scores = dot3(split(jnp.where(mine, q, 0.0)), keys, NT) + bias_of(h)
+        scores = mask_of(scores)
+        weights = jnp.exp(scores - jnp.max(scores, axis=-1, keepdims=True))
+        weights = weights / jnp.sum(weights, axis=-1, keepdims=True)
+        term = dot3(split(weights), split(jnp.where(mine, v, 0.0)))
+        mixture = term if mixture is None else mixture + term
+    return x + dot3(split(jax.nn.sigmoid(g) * mixture), split(out_w[...]))
+
+
+def block_kernel(
+    local,
+    branches,
+    shares,
+    heads,
+    heads_z,
+    right_ref,
+    left_ref,
+    outer_ref,
+    bias_ref,
+    msa_ref,
+    pair_ref,
+    depth_ref,
+    row_proj,
+    row_out,
+    start_proj,
+    start_w,
+    start_out,
+    end_proj,
+    end_w,
+    end_out,
+    msa_o,
+    pair_o,
+    right_all,
+    bias_all,
+    seq_in,
+    seq_res,
+    part_out,
+    part_in,
+    pair_one,
+    start_send,
+    start_all,
+    tile_send,
+    tile_all,
+    column_in,
+    pair_send,
+    own_sem,
+    ag_send,
+    ag_recv,
+    x_send,
+    x_recv,
+    c_send,
+    c_recv,
+    in_send,
+    in_recv,
+    out_send,
+    out_recv,
+    y_send,
+    y_recv,
+    s_send,
+    s_recv,
+    t_send,
+    t_recv,
+    p_send,
+    p_recv,
+):
+    b = lax.axis_index("branch")
+    r = lax.axis_index("res")
+    everyone = branches * shares
+    me = r * branches + b
+    mine = local // branches
+    per_seq = seq_in.shape[0]
+    padded = right_ref.shape[1]
+    residues = shares * padded
+    factors = left_ref.shape[1]
+    half = right_ref.shape[0]
+    outers = shares // 4
+    outer, inner = r // 4, r % 4
+    twin_x = outer * 4 + (inner + 2) % 4
+    twin_c = outer * 4 + (inner // 2) * 2 + (inner + 1) % 2
+    my_rows = r * padded + b * mine
+
+    def remote(src, dst, send, recv, branch, res):
+        return pltpu.make_async_remote_copy(
+            src_ref=src,
+            dst_ref=dst,
+            send_sem=send,
+            recv_sem=recv,
+            device_id={"branch": branch, "res": res},
+            device_id_type=MESH,
+        )
+
+    def each(low, high, body):
+        def step(k, carry):
+            body(k)
+            return carry
+
+        lax.fori_loop(low, high, step, 0)
+
+    start_all[...] = jnp.zeros_like(start_all)
+    tile_all[...] = jnp.zeros_like(tile_all)
+
+    barrier = pltpu.get_barrier_semaphore()
+
+    def greet(k):
+        other = (me + k) % everyone
+        pl.semaphore_signal(
+            barrier,
+            inc=1,
+            device_id={"branch": other % branches, "res": other // branches},
+            device_id_type=MESH,
+        )
+
+    each(1, everyone, greet)
+    pl.semaphore_wait(barrier, everyone - 1)
+
+    pairs = ((right_ref, right_all, 0), (bias_ref, bias_all, 1))
+
+    def stage_one(k, which):
+        source, target, n = which
+        peer = ((outer + k) % outers) * 4 + inner
+        return remote(source, target.at[r], ag_send.at[n, k], ag_recv.at[n, k], b, peer)
+
+    def stage_two(k, which):
+        _, target, n = which
+        at = ((outer + outers - k) % outers) * 4 + inner
+        return remote(
+            target.at[at], target.at[at], x_send.at[n, k], x_recv.at[n, k], b, twin_x
+        )
+
+    def stage_three(k, side, which):
+        _, target, n = which
+        at = ((outer + outers - k) % outers) * 4 + (inner + 2 * side) % 4
+        return remote(
+            target.at[at],
+            target.at[at],
+            c_send.at[n, side, k],
+            c_recv.at[n, side, k],
+            b,
+            twin_c,
+        )
+
+    def seq_copy(k):
+        peer = (r + k) % shares
+        return remote(
+            msa_ref.at[pl.ds(peer * per_seq, per_seq)],
+            seq_in.at[:, r],
+            in_send.at[k],
+            in_recv.at[k],
+            b,
+            peer,
+        )
+
+    own = [
+        pltpu.make_async_copy(right_ref, right_all.at[r], own_sem.at[0]),
+        pltpu.make_async_copy(bias_ref, bias_all.at[r], own_sem.at[1]),
+        pltpu.make_async_copy(
+            msa_ref.at[pl.ds(r * per_seq, per_seq)], seq_in.at[:, r], own_sem.at[2]
+        ),
+    ]
+    for copy in own:
+        copy.start()
+    for which in pairs:
+        each(1, outers, lambda k: stage_one(k, which).start())
+    for copy in own:
+        copy.wait()
+    for which in pairs:
+        stage_two(0, which).start()
+        stage_three(0, 0, which).start()
+    each(1, shares, lambda k: seq_copy(k).start())
+    for which in pairs:
+
+        def forward(k):
+            stage_one(k, which).wait()
+            stage_two(k, which).start()
+            stage_three(k, 0, which).start()
+
+        each(1, outers, forward)
+    for which in pairs:
+
+        def forward_x(k):
+            stage_two(k, which).wait()
+            stage_three(k, 1, which).start()
+
+        each(0, outers, forward_x)
+    for which in pairs:
+
+        def finish(k):
+            stage_three(k, 0, which).wait()
+            stage_three(k, 1, which).wait()
+
+        each(0, outers, finish)
+
+    other_b = (b + 1) % branches
+    left = jnp.concatenate(
+        [left_ref[pl.ds(other_b * mine, mine)], left_ref[pl.ds(b * mine, mine)]], axis=0
+    ).reshape(local * factors, left_ref.shape[2])
+    left = split(left)
+    weight = split(outer_ref[...])
+    products = []
+    for e in range(half):
+        right = split(right_all[:, e].reshape(residues, right_all.shape[3]))
+        products.append(dot3(left, right, NT))
+
+    def outer_row(i):
+        block = jnp.concatenate(
+            [one[i * factors : (i + 1) * factors] for one in products], axis=0
+        )
+        return jnp.transpose(dot3(weight, split(block)))
+
+    for i in range(mine):
+        part_out[i] = outer_row(i)
+    swap = remote(part_out, part_in, y_send, y_recv, other_b, r)
+    swap.start()
+    for i in range(mine):
+        pair_one[i] = outer_row(mine + i)
+
+    depth = jnp.sum(bias_all[:, local, 0, :], axis=0, keepdims=True)
+    depth_rows = jnp.transpose(jnp.broadcast_to(depth, (residues, residues)))
+    lane = lax.broadcasted_iota(jnp.int32, (1, residues), 1)
+    dead = jnp.where(lane % padded < local, masked_score, 3.0 * masked_score)
+    present = depth > 0.5
+
+    def pair_mask(scores):
+        return jnp.where(present, scores, dead)
+
+    first_seq = ((b * shares + r) * per_seq).astype(jnp.float32)
+
+    def row_sequence(s):
+        live = depth > first_seq + s.astype(jnp.float32)
+        x = seq_in[s].reshape(residues, seq_in.shape[3])
+        seq_res[s] = rows_attention(
+            x,
+            lambda h: bias_all[:, :, h, :].reshape(residues, residues),
+            lambda scores: jnp.where(live, scores, dead),
+            row_proj,
+            row_out,
+            heads,
+        )
+
+    swap.wait()
+    for i in range(mine):
+        update = pair_one[i] + part_in[i]
+        overlap = jnp.maximum(jnp.minimum(depth_rows, depth_ref[i]), 1.0)
+        pair_one[i] = pair_ref[i] + update / overlap
+        start_send[i] = dot3(
+            split(start_w[...]), split(layer_normalize(pair_one[i])), NT
+        )[:heads_z]
+
+    def start_copy(k):
+        other = (me + k) % everyone
+        return remote(
+            start_send,
+            start_all.at[pl.ds(my_rows, mine)],
+            s_send.at[k],
+            s_recv.at[k],
+            other % branches,
+            other // branches,
+        )
+
+    each(1, everyone, lambda k: start_copy(k).start())
+    own = pltpu.make_async_copy(
+        start_send, start_all.at[pl.ds(my_rows, mine)], own_sem.at[0]
+    )
+    own.start()
+
+    each(1, shares, lambda k: seq_copy(k).wait())
+    each(0, per_seq // 2, row_sequence)
+
+    own.wait()
+    each(1, everyone, lambda k: start_copy(k).wait())
+
+    for i in range(mine):
+        two = rows_attention(
+            pair_one[i],
+            lambda h: start_all[:, h, :],
+            pair_mask,
+            start_proj,
+            start_out,
+            heads_z,
+        )
+        rows = dot3(split(end_w[...]), split(layer_normalize(two)), NT)[:heads_z]
+        for d in range(everyone):
+            at = (d // branches) * padded + (d % branches) * mine
+            tile_send[d, i, :mine] = two[at : at + mine]
+            tile_send[d, i, mine : mine + heads_z] = rows
+
+    def tile_copy(k):
+        other = (me + k) % everyone
+        return remote(
+            tile_send.at[other],
+            tile_all.at[pl.ds(my_rows, mine)],
+            t_send.at[k],
+            t_recv.at[k],
+            other % branches,
+            other // branches,
+        )
+
+    each(1, everyone, lambda k: tile_copy(k).start())
+    own = pltpu.make_async_copy(
+        tile_send.at[me], tile_all.at[pl.ds(my_rows, mine)], own_sem.at[0]
+    )
+    own.start()
+    each(per_seq // 2, per_seq, row_sequence)
+
+    def row_copy(k):
+        peer = (r + k) % shares
+        return remote(
+            seq_res.at[:, pl.ds(pl.multiple_of(peer * padded, padded), padded), :],
+            msa_o.at[pl.ds(r * per_seq, per_seq)],
+            out_send.at[k],
+            out_recv.at[k],
+            b,
+            peer,
+        )
+
+    own.wait()
+    each(1, everyone, lambda k: tile_copy(k).wait())
+    each(1, shares, lambda k: row_copy(k).start())
+    own_row = pltpu.make_async_copy(
+        seq_res.at[:, pl.ds(pl.multiple_of(r * padded, padded), padded), :],
+        msa_o.at[pl.ds(r * per_seq, per_seq)],
+        own_sem.at[1],
+    )
+    own_row.start()
+
+    width = pair_ref.shape[2]
+    share = width // branches
+    for h in range(heads_z):
+        column_in[h] = jnp.transpose(tile_all[:, mine + h, :])
+    results = []
+    for i in range(mine):
+        results.append(
+            rows_attention(
+                tile_all[:, i, :],
+                lambda h: column_in[h],
+                pair_mask,
+                end_proj,
+                end_out,
+                heads_z,
+            )
+        )
+    for c in range(branches):
+        pair_send[c] = jnp.concatenate(
+            [one[:, c * share : (c + 1) * share] for one in results]
+            + [jnp.zeros((residues, pair_send.shape[2] - mine * share), jnp.float32)],
+            axis=1,
+        )
+
+    def pair_copy(k):
+        other = (me + k) % everyone
+        at = pl.multiple_of((other // branches) * padded, padded)
+        return remote(
+            pair_send.at[other % branches, pl.ds(at, padded), :],
+            pair_o.at[me],
+            p_send.at[k],
+            p_recv.at[k],
+            other % branches,
+            other // branches,
+        )
+
+    each(1, everyone, lambda k: pair_copy(k).start())
+    own = pltpu.make_async_copy(
+        pair_send.at[b, pl.ds(pl.multiple_of(r * padded, padded), padded), :],
+        pair_o.at[me],
+        own_sem.at[0],
+    )
+    own.start()
+    own.wait()
+    own_row.wait()
+    each(1, shares, lambda k: row_copy(k).wait())
+    each(1, everyone, lambda k: pair_copy(k).wait())
+
+
+def fused(
+    msa, pair, msa_mask, row_proj, row_out, row_bias_w, first_w, other_w, outer_w,
+    start_proj, start_bias_w, start_out, end_proj, end_bias_w, end_out, padded,
+):
+    b = lax.axis_index("branch")
+    r = lax.axis_index("res")
+    branches = lax.axis_size("branch")
+    shares = lax.axis_size("res")
+    everyone = branches * shares
+    sequences, local, features = msa.shape
+    residues, width = pair.shape[1:]
+    factors = first_w.shape[1]
+    half = factors // branches
+    mine = local // branches
+    per_seq = sequences // everyone
+    spread = shares * padded
+    heads, heads_z = row_bias_w.shape[1], start_bias_w.shape[1]
+    spare = padded - local
+
+    depth = jnp.sum(msa_mask, axis=0).astype(jnp.float32)
+    wide = jnp.pad(
+        pair.reshape(local, shares, local, width), ((0, 0), (0, 0), (0, spare), (0, 0))
+    ).reshape(local, spread, width)
+    bias_rows = project(layer_normalize(wide), row_bias_w, "ijc,ch->ihj")
+    placed = lax.dynamic_update_slice(jnp.zeros((spread,), jnp.float32), depth, (r * padded,))
+    bias_pack = jnp.concatenate(
+        [bias_rows, jnp.broadcast_to(placed, (spare, heads, spread))], axis=0
+    )
+    normed = layer_normalize(msa)
+    my_other = lax.dynamic_slice_in_dim(other_w, b * half, half, axis=1)
+    mask = jnp.transpose(msa_mask).astype(jnp.float32)
+    left = project(normed, first_w, "sia,ac->ics") * mask[:, None, :]
+    right = project(normed, my_other, "sja,ae->ejs") * mask[None]
+    right = jnp.pad(right, ((0, 0), (0, spare), (0, 0)))
+    part = sequences // branches
+    my_msa = lax.dynamic_slice_in_dim(msa, b * part, part, axis=0)
+    my_msa = jnp.pad(my_msa, ((0, 0), (0, spare), (0, 0)))
+    weight = outer_w.reshape(factors, factors, width)
+    weight = lax.dynamic_slice_in_dim(weight, b * half, half, axis=1)
+    weight = jnp.transpose(weight, (2, 1, 0)).reshape(width, half * factors)
+    my_pair = lax.dynamic_slice_in_dim(wide, b * mine, mine)
+    my_depth = lax.dynamic_slice_in_dim(depth, b * mine, mine)
+    my_depth = jnp.broadcast_to(my_depth[:, None, None], (mine, 1, width))
+    start_w = jnp.pad(jnp.transpose(start_bias_w), ((0, -heads_z % 8), (0, 0)))
+    end_w = jnp.pad(jnp.transpose(end_bias_w), ((0, -heads_z % 8), (0, 0)))
+
+    outers = shares // 4
+    lanes = -(-(mine * (width // branches)) // 128) * 128
+    stack = -(-(mine + heads_z) // 8) * 8
+    f32 = jnp.float32
+    dma = pltpu.SemaphoreType.DMA
+    vmem = pl.BlockSpec(memory_space=pltpu.VMEM)
+    args = (
+        right, left, weight, bias_pack, my_msa, my_pair, my_depth, row_proj, row_out,
+        start_proj, start_w, start_out, end_proj, end_w, end_out,
+    )
+    msa_o, pair_o = pl.pallas_call(
+        functools.partial(block_kernel, local, branches, shares, heads, heads_z),
+        out_shape=(
+            jax.ShapeDtypeStruct((part, padded, features), f32),
+            jax.ShapeDtypeStruct((everyone, padded, lanes), f32),
+        ),
+        in_specs=[vmem] * len(args),
+        out_specs=(vmem, vmem),
+        scratch_shapes=[
+            pltpu.VMEM((shares,) + right.shape, f32),
+            pltpu.VMEM((shares,) + bias_pack.shape, f32),
+            pltpu.VMEM((per_seq, shares, padded, features), f32),
+            pltpu.VMEM((per_seq, spread, features), f32),
+            pltpu.VMEM((mine, spread, width), f32),
+            pltpu.VMEM((mine, spread, width), f32),
+            pltpu.VMEM((mine, spread, width), f32),
+            pltpu.VMEM((mine, heads_z, spread), f32),
+            pltpu.VMEM((spread, heads_z, spread), f32),
+            pltpu.VMEM((everyone, mine, stack, width), f32),
+            pltpu.VMEM((spread, stack, width), f32),
+            pltpu.VMEM((heads_z, spread, spread), f32),
+            pltpu.VMEM((branches, spread, lanes), f32),
+            dma((3,)),
+            dma((2, outers)),
+            dma((2, outers)),
+            dma((2, outers)),
+            dma((2, outers)),
+            dma((2, 2, outers)),
+            dma((2, 2, outers)),
+            dma((shares,)),
+            dma((shares,)),
+            dma((shares,)),
+            dma((shares,)),
+            dma,
+            dma,
+            dma((everyone,)),
+            dma((everyone,)),
+            dma((everyone,)),
+            dma((everyone,)),
+            dma((everyone,)),
+            dma((everyone,)),
+        ],
+        compiler_params=pltpu.CompilerParams(
+            collective_id=0, has_side_effects=True, vmem_limit_bytes=56 * 1024 * 1024
+        ),
+    )(*args)
+    piece = width // branches
+    pair_o = pair_o[:, :local, : mine * piece].reshape(everyone, local, mine, piece)
+    pair_o = jnp.transpose(pair_o, (1, 0, 2, 3)).reshape(local, residues, piece)
+    return msa_o[:, :local], pair_o
 
 
 def per_device(
@@ -161,6 +656,12 @@
     half = factors // branches
     mine = local // branches
     per_seq = sequences // everyone
+    room = -(-(local + 1) // 8) * 8
+    if shares * room == width and shares % 4 == 0 and width == 128:
+        return fused(
+            msa, pair, msa_mask, row_proj, row_out, row_bias_w, first_w, other_w, outer_w,
+            start_proj, start_bias_w, start_out, end_proj, end_bias_w, end_out, room,
+        )
     padded = -(-local // 8) * 8
 
     depth = jnp.sum(msa_mask, axis=0).astype(jnp.float32)

time: 177 us -> 99.3 us (0.56)
  waiting for transfers between devices: 69.3 us -> 0 us
  Pallas kernels: 31.5 us -> 82.7 us
  starting transfers between devices: 40.2 us -> 0 us
  local copies, waits for them, and re-layouts: 26.6 us -> 11.3 us
  other arithmetic: 4.97 us -> 1.87 us
    all_to_all x9 -> x0, waiting for transfers between devices: 69.3 us -> none  [the longest x4 40.8 us: gather(): return lax.all_to_all(copies, axes, 0, 0)]
    pallas_call x4 -> x1, Pallas kernels: 31.5 us -> 82.7 us  [fused(): pl.pallas_call(functools.partial(block_kernel, local, branches, shares, h...]
    all_to_all x9 -> x0, starting transfers between devices: 40.2 us -> none  [the longest x4 19.9 us: gather(): return lax.all_to_all(copies, axes, 0, 0)]
    reshape x9 -> x4, local copies, waits for them, and re-layouts: 5.77 us -> 2.19 us  [the longest x1 1.06 us: fused(): pair.reshape(local, shares, local, width)]
    broadcast_in_dim x6 -> x3, local copies, waits for them, and re-layouts: 4.03 us -> 0.59 us  [the longest x1 0.59 us: fused(): my_depth = jnp.broadcast_to(my_depth[:, None, None], (mine, 1, width))]
    all_to_all x8 -> x0, local copies, waits for them, and re-layouts: 3.38 us -> none  [the longest x2 0.97 us: per_device(): lax.all_to_all(my_msa, 'res', split_axis=0, concat_axis=1, tiled=True)]
    unnamed x28 -> x21, local copies, waits for them, and re-layouts: 7.02 us -> 3.75 us
    another operation x3 -> x0, local copies, waits for them, and re-layouts: 2.5 us -> none  [the longest x2 1.78 us: per_device(): lax.all_to_all(pair_two.reshape(mine, everyone, mine, width), EVERYONE, 1...]
  transfers between devices with their start and end apart: 9 -> 0, of which waited for: 8 -> 0; matrix products, arithmetic and copies ran while one was open for 11% -> 0% of each run, Pallas kernels for 16% -> 0%
where the time goes in v2:
time: 99.3 us; the launch traced here: 98.9 us
  Pallas kernels  82.7 us (83%)
  local copies, waits for them, and re-layouts  11.3 us (11%)
  matrix products  2.3 us (2%)
  other arithmetic  1.87 us (2%)
    pallas_call x1, Pallas kernels, fused(): pl.pallas_call(functools.partial(block_kernel, local, branches, shares, h...  82.7 us
    unnamed x21, local copies, waits for them, and re-layouts  3.75 us
    dot_general x3, matrix products, project(): return jnp.einsum(form, a, b, precision=lax.Precision.HIGH)  2.3 us

profile of v2, /device:TPU:0, one launch (start us, length us, event | category | flops | bytes accessed | tf_op | source)
XLA Modules:
  0.0 98.9 jit_solution(12810551281404502598)
XLA Ops:
  0.6 0.0 copy-start
  0.6 1.1 %reshape.70 = f32[6,16,6,128]{3,2,1,0:T(8,128)S(1)} reshape(f32[6,96,128]{2,1,0:T(8,128)} %param.17) | data formatting | bytes 589824 | tf_op jit(solution)/shard_map/reshape | solution.py:544
  1.7 0.2 pad_bitcast_fusion
  1.9 0.0 copy-start.1
  1.9 0.3 multiply_reduce_fusion.1
  2.3 0.1 rsqrt.21
  2.4 0.0 copy-start.5
  2.4 0.1 div.17
  2.5 0.6 copy-done.5
  3.0 0.5 convolution_bitcast_fusion.1
  3.5 0.0 copy-start.6
  3.5 0.7 copy-done.6
  4.2 0.1 fusion.19
  4.3 0.1 convert_dynamic-update-slice_fusion
  4.4 0.6 pad_maximum_fusion.bias_ref
  5.1 0.0 copy-done.1
  5.1 0.2 reduce_sum.45
  5.3 0.0 copy-start.4
  5.3 0.3 multiply_reduce_fusion
  5.6 0.4 copy-done.4
  6.0 0.6 fusion.2
  6.6 0.6 pad.19.right_ref
  7.3 0.7 constant_dynamic-slice_fusion.pair_ref
  8.0 0.1 dynamic_slice.19
  8.0 0.6 broadcast_in_dim.8.depth_ref
  8.6 0.0 copy-done
  8.6 0.1 copy.29
  8.7 0.8 copy.31.outer_ref
  9.6 0.2 copy.35
  9.9 0.0 copy-start.3
  9.9 0.8 pad.21.msa_ref
  10.7 0.0 copy-done.3
  10.7 0.0 copy-start.7
  10.7 0.0 copy-start.8
  10.7 1.2 %fusion.left_ref = f32[6,32,128]{2,1,0:T(8,128)} fusion(f32[128,6,256]{2,0,1:T(8,128)S(1)} %copy-done.1, f32[128,6]{0,1:T(8,128)S(1)} %add_rsqrt_fusion.1, f32[128,6]{0,1:T(8,128)S(1)} %broadcast_multiply_fusion.1, f32[6,128]{1,0:T(8,128)S(1)} %get-tuple-element.15, f32[256,32]{0,1:T(8,128)S(1)} %copy-done.3), kind=kOutput, calls=%fused_computation.1 | convolution fusion | flops 38166528 | bytes 926720 | tf_op jit(solution)/shard_map/sia,ac->ics/dot_general | solution.py:128
  12.0 0.0 copy-done.7
  12.0 0.6 pad.22.start_w
  12.6 0.0 copy-done.8
  12.6 0.6 pad.23.end_w
  13.1 82.7 %shard_map.158 = (f32[64,8,256]{2,1,0:T(8,128)}, f32[32,8,256]{2,1,0:T(8,128)}) custom-call(f32[16,8,128]{2,1,0:T(8,128)} %pad.19.right_ref, f32[6,32,128]{2,1,0:T(8,128)} %fusion.left_ref, f32[128,512]{1,0:T(8,128)} %copy.31.outer_ref, f32[8,8,128]{2,1,0:T(8,128)} %pad_maximum_fusion.bias_ref, f32[64,8,256]{2,1,0:T(8,128)} %pad.21.msa_ref, ...), custom_call_target="tpu_custom_call" | custom-call | tf_op jit(solution)/shard_map/pallas_call | solution.py:579
  95.8 1.0 %copy.32 = f32[32,6,192]{2,0,1:T(8,128)S(1)} copy(f32[32,6,192]{2,1,0:T(8,128)} %bitcast.39) | data formatting | bytes 294912 | tf_op jit(solution)/shard_map/slice | solution.py:626
  96.8 0.2 reshape.72
  97.0 0.0 copy-start.2
  97.0 0.1 reshape.73
  97.2 0.8 copy.34
  98.0 0.1 copy-done.2
  98.0 0.9 copy.33
  (10 shorter events, 0.1 us)
Async XLA Ops:
  0.6 8.0 %copy-start = (f32[1024,128]{1,0:T(8,128)S(1)}, f32[1024,128]{1,0:T(8,128)}, u32[]{:S(2)}) copy-start(f32[1024,128]{1,0:T(8,128)} %param.24) | copy-start | bytes 1572868
  1.9 3.2 %copy-start.1 = (f32[128,6,256]{2,0,1:T(8,128)S(1)}, f32[128,6,256]{2,0,1:T(8,128)}, u32[]{:S(2)}) copy-start(f32[128,6,256]{2,0,1:T(8,128)} %param.16) | copy-start | bytes 2359300
  2.4 0.7 copy-start.5
  3.5 0.7 copy-start.6
  5.3 0.8 copy-start.4
  9.9 0.8 copy-start.3
  10.7 1.3 %copy-start.7 = (f32[128,4]{0,1:T(4,128)S(1)}, f32[128,4]{0,1:T(4,128)}, u32[]{:S(2)}) copy-start(f32[128,4]{0,1:T(4,128)} %param.26) | copy-start | bytes 6148
  10.7 1.9 %copy-start.8 = (f32[128,4]{0,1:T(4,128)S(1)}, f32[128,4]{0,1:T(4,128)}, u32[]{:S(2)}) copy-start(f32[128,4]{0,1:T(4,128)} %param.29) | copy-start | bytes 6148
  97.0 1.0 %copy-start.2 = (f32[64,8,256]{2,1,0:T(8,128)S(1)}, f32[64,8,256]{2,1,0:T(8,128)}, u32[]{:S(2)}) copy-start(f32[64,8,256]{2,1,0:T(8,128)} %get-tuple-element.4) | copy-start | bytes 1572868

commit v3 on v2

--- a/solution.py
+++ b/solution.py
@@ -137,22 +137,67 @@
 
 
 def rows_attention(x, bias_of, mask_of, proj, out_w, heads):
-    channels = x.shape[1]
+    lines, channels = x.shape
     width = channels // heads
+    tile = 128
+    per_tile = tile // width
     normed = split(layer_normalize(x))
     q, k, v, g = (dot3(normed, split(proj[p])) for p in range(4))
     q = q * (1.0 / math.sqrt(width))
-    keys = split(k)
-    owner = lax.broadcasted_iota(jnp.int32, (1, channels), 1) // width
-    mixture = None
-    for h in range(heads):
-        mine = owner == h
-        scores = dot3(split(jnp.where(mine, q, 0.0)), keys, NT) + bias_of(h)
-        scores = mask_of(scores)
-        weights = jnp.exp(scores - jnp.max(scores, axis=-1, keepdims=True))
-        weights = weights / jnp.sum(weights, axis=-1, keepdims=True)
-        term = dot3(split(weights), split(jnp.where(mine, v, 0.0)))
-        mixture = term if mixture is None else mixture + term
+    owner = lax.broadcasted_iota(jnp.int32, (1, tile), 1) // width
+    bf16 = jnp.bfloat16
+    mixtures = []
+    for first in range(0, channels, tile):
+
+        def halves(values):
+            values = values[:, first : first + tile]
+            high = values.astype(bf16).astype(jnp.float32)
+            return high, values - high
+
+        (q_hi, q_lo), (k_hi, k_lo), (v_hi, v_lo) = halves(q), halves(k), halves(v)
+        q_turn = pltpu.roll(q_hi, width, 1)
+        k_turn = pltpu.roll(k_lo, width, 1)
+        keys = [
+            jnp.concatenate(
+                [k_hi, jnp.where(owner % 2 == parity, k_hi, k_turn)], axis=1
+            ).astype(bf16)
+            for parity in range(2)
+        ]
+        total = None
+        for n in range(per_tile):
+            mine, after = owner == n, owner == (n + 1) % per_tile
+            query = jnp.concatenate(
+                [
+                    jnp.where(mine, q_hi, 0.0),
+                    jnp.where(mine, q_lo, jnp.where(after, q_turn, 0.0)),
+                ],
+                axis=1,
+            ).astype(bf16)
+            scores = lax.dot_general(
+                query, keys[n % 2], NT, preferred_element_type=jnp.float32
+            )
+            scores = mask_of(scores + bias_of(first // width + n))
+            weights = jnp.exp(scores - jnp.max(scores, axis=-1, keepdims=True))
+            weights = weights / jnp.sum(weights, axis=-1, keepdims=True)
+            w_hi, w_lo = split(weights)
+            m_hi = jnp.where(mine, v_hi, 0.0).astype(bf16)
+            m_lo = jnp.where(mine, v_lo, 0.0).astype(bf16)
+            values = jnp.concatenate(
+                [
+                    jnp.concatenate([m_hi, m_lo], axis=1),
+                    jnp.concatenate([m_hi, jnp.zeros_like(m_lo)], axis=1),
+                ],
+                axis=0,
+            )
+            term = lax.dot_general(
+                jnp.concatenate([w_hi, w_lo], axis=1),
+                values,
+                NN,
+                preferred_element_type=jnp.float32,
+            )
+            total = term if total is None else total + term
+        mixtures.append(total[:, :tile] + total[:, tile:])
+    mixture = mixtures[0] if len(mixtures) == 1 else jnp.concatenate(mixtures, axis=1)
     return x + dot3(split(jax.nn.sigmoid(g) * mixture), split(out_w[...]))
 
 
@@ -162,13 +207,13 @@
     shares,
     heads,
     heads_z,
-    right_ref,
-    left_ref,
+    msa_ref,
+    mask_ref,
+    wide_ref,
+    place_ref,
+    factor_w,
+    bias_w,
     outer_ref,
-    bias_ref,
-    msa_ref,
-    pair_ref,
-    depth_ref,
     row_proj,
     row_out,
     start_proj,
@@ -179,6 +224,11 @@
     end_out,
     msa_o,
     pair_o,
+    left_ref,
+    right_ref,
+    bias_ref,
+    pair_ref,
+    seq_pad,
     right_all,
     bias_all,
     seq_in,
@@ -247,6 +297,10 @@
 
     start_all[...] = jnp.zeros_like(start_all)
     tile_all[...] = jnp.zeros_like(tile_all)
+    right_ref[...] = jnp.zeros_like(right_ref)
+    bias_ref[...] = jnp.zeros_like(bias_ref)
+    seq_pad[...] = jnp.zeros_like(seq_pad)
+    pair_ref[...] = jnp.zeros_like(pair_ref)
 
     barrier = pltpu.get_barrier_semaphore()
 
@@ -260,6 +314,22 @@
         )
 
     each(1, everyone, greet)
+
+    factor = split(factor_w[...])
+    for j in range(local):
+        line = split(layer_normalize(msa_ref[:, j, :]))
+        both = dot3(factor, line, NT) * mask_ref[j : j + 1]
+        left_ref[j] = both[:factors]
+        right_ref[:, j, :] = both[factors:]
+    for i in range(local):
+        for share in range(shares):
+            pair_ref[i, share * padded : share * padded + local, :] = wide_ref[
+                i, share * local : (share + 1) * local, :
+            ]
+    weight = split(bias_w[...])
+    for i in range(local):
+        bias_ref[i] = dot3(weight, split(layer_normalize(pair_ref[i])), NT)
+    bias_ref[local] = jnp.broadcast_to(place_ref[...], bias_ref.shape[1:])
     pl.semaphore_wait(barrier, everyone - 1)
 
     pairs = ((right_ref, right_all, 0), (bias_ref, bias_all, 1))
@@ -291,7 +361,7 @@
     def seq_copy(k):
         peer = (r + k) % shares
         return remote(
-            msa_ref.at[pl.ds(peer * per_seq, per_seq)],
+            msa_ref.at[pl.ds((b * shares + peer) * per_seq, per_seq)],
             seq_in.at[:, r],
             in_send.at[k],
             in_recv.at[k],
@@ -303,7 +373,7 @@
         pltpu.make_async_copy(right_ref, right_all.at[r], own_sem.at[0]),
         pltpu.make_async_copy(bias_ref, bias_all.at[r], own_sem.at[1]),
         pltpu.make_async_copy(
-            msa_ref.at[pl.ds(r * per_seq, per_seq)], seq_in.at[:, r], own_sem.at[2]
+            msa_ref.at[pl.ds((b * shares + r) * per_seq, per_seq)], seq_in.at[:, r], own_sem.at[2]
         ),
     ]
     for copy in own:
@@ -376,7 +446,8 @@
 
     def row_sequence(s):
         live = depth > first_seq + s.astype(jnp.float32)
-        x = seq_in[s].reshape(residues, seq_in.shape[3])
+        seq_pad[:, :local, :] = seq_in[s]
+        x = seq_pad[...].reshape(residues, seq_in.shape[3])
         seq_res[s] = rows_attention(
             x,
             lambda h: bias_all[:, :, h, :].reshape(residues, residues),
@@ -386,14 +457,15 @@
             heads,
         )
 
+    column_in[0] = depth_rows
     swap.wait()
     for i in range(mine):
         update = pair_one[i] + part_in[i]
-        overlap = jnp.maximum(jnp.minimum(depth_rows, depth_ref[i]), 1.0)
-        pair_one[i] = pair_ref[i] + update / overlap
+        overlap = jnp.maximum(jnp.minimum(depth_rows, column_in[0, pl.ds(my_rows + i, 1), :]), 1.0)
+        pair_one[i] = pair_ref[b * mine + i] + update / overlap
         start_send[i] = dot3(
             split(start_w[...]), split(layer_normalize(pair_one[i])), NT
-        )[:heads_z]
+        )
 
     def start_copy(k):
         other = (me + k) % everyone
@@ -427,7 +499,7 @@
             start_out,
             heads_z,
         )
-        rows = dot3(split(end_w[...]), split(layer_normalize(two)), NT)[:heads_z]
+        rows = dot3(split(end_w[...]), split(layer_normalize(two)), NT)
         for d in range(everyone):
             at = (d // branches) * padded + (d % branches) * mine
             tile_send[d, i, :mine] = two[at : at + mine]
@@ -537,34 +609,18 @@
     per_seq = sequences // everyone
     spread = shares * padded
     heads, heads_z = row_bias_w.shape[1], start_bias_w.shape[1]
-    spare = padded - local
-
-    depth = jnp.sum(msa_mask, axis=0).astype(jnp.float32)
-    wide = jnp.pad(
-        pair.reshape(local, shares, local, width), ((0, 0), (0, 0), (0, spare), (0, 0))
-    ).reshape(local, spread, width)
-    bias_rows = project(layer_normalize(wide), row_bias_w, "ijc,ch->ihj")
-    placed = lax.dynamic_update_slice(jnp.zeros((spread,), jnp.float32), depth, (r * padded,))
-    bias_pack = jnp.concatenate(
-        [bias_rows, jnp.broadcast_to(placed, (spare, heads, spread))], axis=0
-    )
-    normed = layer_normalize(msa)
+
+    mask = jnp.transpose(msa_mask).astype(jnp.float32)
+    depth = jnp.sum(mask, axis=1)
+    place = lax.dynamic_update_slice(
+        jnp.zeros((1, spread), jnp.float32), depth[None], (0, r * padded)
+    )
     my_other = lax.dynamic_slice_in_dim(other_w, b * half, half, axis=1)
-    mask = jnp.transpose(msa_mask).astype(jnp.float32)
-    left = project(normed, first_w, "sia,ac->ics") * mask[:, None, :]
-    right = project(normed, my_other, "sja,ae->ejs") * mask[None]
-    right = jnp.pad(right, ((0, 0), (0, spare), (0, 0)))
+    factor_w = jnp.transpose(jnp.concatenate([first_w, my_other], axis=1))
     part = sequences // branches
-    my_msa = lax.dynamic_slice_in_dim(msa, b * part, part, axis=0)
-    my_msa = jnp.pad(my_msa, ((0, 0), (0, spare), (0, 0)))
     weight = outer_w.reshape(factors, factors, width)
     weight = lax.dynamic_slice_in_dim(weight, b * half, half, axis=1)
     weight = jnp.transpose(weight, (2, 1, 0)).reshape(width, half * factors)
-    my_pair = lax.dynamic_slice_in_dim(wide, b * mine, mine)
-    my_depth = lax.dynamic_slice_in_dim(depth, b * mine, mine)
-    my_depth = jnp.broadcast_to(my_depth[:, None, None], (mine, 1, width))
-    start_w = jnp.pad(jnp.transpose(start_bias_w), ((0, -heads_z % 8), (0, 0)))
-    end_w = jnp.pad(jnp.transpose(end_bias_w), ((0, -heads_z % 8), (0, 0)))
 
     outers = shares // 4
     lanes = -(-(mine * (width // branches)) // 128) * 128
@@ -573,8 +629,9 @@
     dma = pltpu.SemaphoreType.DMA
     vmem = pl.BlockSpec(memory_space=pltpu.VMEM)
     args = (
-        right, left, weight, bias_pack, my_msa, my_pair, my_depth, row_proj, row_out,
-        start_proj, start_w, start_out, end_proj, end_w, end_out,
+        msa, mask, pair, place, factor_w, jnp.transpose(row_bias_w), weight,
+        row_proj, row_out, start_proj, jnp.transpose(start_bias_w), start_out,
+        end_proj, jnp.transpose(end_bias_w), end_out,
     )
     msa_o, pair_o = pl.pallas_call(
         functools.partial(block_kernel, local, branches, shares, heads, heads_z),
@@ -585,9 +642,14 @@
         in_specs=[vmem] * len(args),
         out_specs=(vmem, vmem),
         scratch_shapes=[
-            pltpu.VMEM((shares,) + right.shape, f32),
-            pltpu.VMEM((shares,) + bias_pack.shape, f32),
-            pltpu.VMEM((per_seq, shares, padded, features), f32),
+            pltpu.VMEM((local, factors, sequences), f32),
+            pltpu.VMEM((half, padded, sequences), f32),
+            pltpu.VMEM((padded, heads, spread), f32),
+            pltpu.VMEM((local, spread, width), f32),
+            pltpu.VMEM((shares, padded, features), f32),
+            pltpu.VMEM((shares, half, padded, sequences), f32),
+            pltpu.VMEM((shares, padded, heads, spread), f32),
+            pltpu.VMEM((per_seq, shares, local, features), f32),
             pltpu.VMEM((per_seq, spread, features), f32),
             pltpu.VMEM((mine, spread, width), f32),
             pltpu.VMEM((mine, spread, width), f32),

time: 99.3 us -> 90.4 us (0.910)
  local copies, waits for them, and re-layouts: 11.3 us -> 7.59 us
  matrix products: 2.3 us -> 0 us
  Pallas kernels: 82.7 us -> 80.5 us
    pad x4 -> x0, local copies, waits for them, and re-layouts: 2.64 us -> none  [the longest x1 0.83 us: fused(): my_msa = jnp.pad(my_msa, ((0, 0), (0, spare), (0, 0)))]
    dot_general x3 -> x0, matrix products: 2.3 us -> none  [project(): return jnp.einsum(form, a, b, precision=lax.Precision.HIGH)]
    pallas_call x1, Pallas kernels: 82.7 us -> 80.5 us  [fused(): pl.pallas_call(functools.partial(block_kernel, local, branches, shares, h...]
    unnamed x21 -> x15, local copies, waits for them, and re-layouts: 3.75 us -> 5.42 us
    reshape x1 -> x0, local copies, waits for them, and re-layouts: 1.06 us -> none  [fused(): pair.reshape(local, shares, local, width)]
where the time goes in v3:
time: 90.4 us; the launch traced here: 90.1 us
  Pallas kernels  80.5 us (89%)
  local copies, waits for them, and re-layouts  7.59 us (8%)
  other arithmetic  1.33 us (1%)
    pallas_call x1, Pallas kernels, fused(): pl.pallas_call(functools.partial(block_kernel, local, branches, shares, h...  80.5 us
    unnamed x15, local copies, waits for them, and re-layouts  5.42 us

profile of v3, /device:TPU:0, one launch (start us, length us, event | category | flops | bytes accessed | tf_op | source)
XLA Modules:
  0.0 90.1 jit_solution(5393754966830447418)
XLA Ops:
  0.6 0.0 copy-start
  0.7 0.0 copy-start.4
  0.7 0.0 copy-start.3
  0.7 1.0 %copy-done = f32[1024,128]{1,0:T(8,128)S(1)} copy-done((f32[1024,128]{1,0:T(8,128)S(1)}, f32[1024,128]{1,0:T(8,128)}, u32[]{:S(2)}) %copy-start) | copy-done | bytes 524312
  1.7 0.0 copy-done.4
  1.7 0.1 convert_reduce_fusion
  1.8 0.1 dynamic_update_slice.3.place_ref
  2.0 0.0 copy-start.5
  2.0 0.6 convert_bitcast_fusion.mask_ref
  2.6 0.0 copy-done.5
  2.6 0.7 constant_dynamic-slice_fusion
  3.3 0.0 copy-done.3
  3.3 0.6 maximum_bitcast_fusion.factor_w
  3.9 0.0 copy-start.1
  3.9 0.1 copy.26
  4.0 0.8 copy.28.outer_ref
  4.9 0.2 copy-done.1
  5.0 1.4 %copy.27.msa_ref = f32[128,6,256]{2,1,0:T(8,128)} copy(f32[128,6,256]{2,0,1:T(8,128)S(1)} %copy-done.1) | data formatting | bytes 1572864 | tf_op args[0]
  6.5 80.5 %shard_map.158 = (f32[64,8,256]{2,1,0:T(8,128)}, f32[32,8,256]{2,1,0:T(8,128)}) custom-call(f32[128,6,256]{2,1,0:T(8,128)} %copy.27.msa_ref, f32[6,128]{1,0:T(8,128)} %convert_bitcast_fusion.mask_ref, f32[6,96,128]{2,1,0:T(8,128)} %wide_ref.1, f32[1,128]{1,0:T(1,128)} %copy-done.5, f32[48,256]{1,0:T(8,128)} %maximum_bitcast_fusion.factor_w, ...), custom_call_target="tpu_custom_call" | custom-call | tf_op jit(solution)/shard_map/pallas_call | solution.py:636
  86.9 0.0 copy-start.2
  86.9 2.0 %copy.30 = f32[64,6,256]{2,0,1:T(8,128)} copy(f32[64,6,256]{2,1,0:T(8,128)} %bitcast.20) | data formatting | bytes 786432
  88.9 0.0 copy-done.2
  88.9 0.1 copy.29
  89.0 0.2 reshape.18
  89.1 0.1 reshape.19
  89.3 0.8 copy.31
  (2 shorter events, 0.0 us)
Async XLA Ops:
  0.6 1.0 %copy-start = (f32[1024,128]{1,0:T(8,128)S(1)}, f32[1024,128]{1,0:T(8,128)}, u32[]{:S(2)}) copy-start(f32[1024,128]{1,0:T(8,128)} %param.24) | copy-start | bytes 1572868
  0.7 1.0 %copy-start.4 = (s32[128,6]{0,1:T(8,128)S(1)}, s32[128,6]{0,1:T(8,128)}, u32[]{:S(2)}) copy-start(s32[128,6]{0,1:T(8,128)} %param.18) | copy-start | bytes 9220
  0.7 2.6 %copy-start.3 = (f32[256,32]{0,1:T(8,128)S(1)}, f32[256,32]{0,1:T(8,128)}, u32[]{:S(2)}) copy-start(f32[256,32]{0,1:T(8,128)} %param.22) | copy-start | bytes 98308
  2.0 0.6 copy-start.5
  3.9 1.1 %copy-start.1 = (f32[128,6,256]{2,0,1:T(8,128)S(1)}, f32[128,6,256]{2,0,1:T(8,128)}, u32[]{:S(2)}) copy-start(f32[128,6,256]{2,0,1:T(8,128)} %param.16) | copy-start | bytes 2359300
  86.9 2.0 %copy-start.2 = (f32[32,8,256]{2,1,0:T(8,128)S(1)}, f32[32,8,256]{2,1,0:T(8,128)}, u32[]{:S(2)}) copy-start(f32[32,8,256]{2,1,0:T(8,128)} %get-tuple-element.5) | copy-start | bytes 786436

commit v4 on v3

--- a/solution.py
+++ b/solution.py
@@ -329,7 +329,7 @@
     weight = split(bias_w[...])
     for i in range(local):
         bias_ref[i] = dot3(weight, split(layer_normalize(pair_ref[i])), NT)
-    bias_ref[local] = jnp.broadcast_to(place_ref[...], bias_ref.shape[1:])
+    right_ref[0, local : local + 1, :] = place_ref[...]
     pl.semaphore_wait(barrier, everyone - 1)
 
     pairs = ((right_ref, right_all, 0), (bias_ref, bias_all, 1))
@@ -378,36 +378,34 @@
     ]
     for copy in own:
         copy.start()
-    for which in pairs:
-        each(1, outers, lambda k: stage_one(k, which).start())
-    for copy in own:
-        copy.wait()
-    for which in pairs:
-        stage_two(0, which).start()
-        stage_three(0, 0, which).start()
-    each(1, shares, lambda k: seq_copy(k).start())
-    for which in pairs:
-
-        def forward(k):
+    def forward(which):
+        def one(k):
             stage_one(k, which).wait()
             stage_two(k, which).start()
             stage_three(k, 0, which).start()
 
-        each(1, outers, forward)
-    for which in pairs:
-
-        def forward_x(k):
+        def across(k):
             stage_two(k, which).wait()
             stage_three(k, 1, which).start()
-
-        each(0, outers, forward_x)
-    for which in pairs:
 
         def finish(k):
             stage_three(k, 0, which).wait()
             stage_three(k, 1, which).wait()
 
+        each(1, outers, one)
+        each(0, outers, across)
         each(0, outers, finish)
+
+    each(1, outers, lambda k: stage_one(k, pairs[0]).start())
+    for copy in own:
+        copy.wait()
+    stage_two(0, pairs[0]).start()
+    stage_three(0, 0, pairs[0]).start()
+    forward(pairs[0])
+    each(1, outers, lambda k: stage_one(k, pairs[1]).start())
+    stage_two(0, pairs[1]).start()
+    stage_three(0, 0, pairs[1]).start()
+    each(1, shares, lambda k: seq_copy(k).start())
 
     other_b = (b + 1) % branches
     left = jnp.concatenate(
@@ -433,7 +431,7 @@
     for i in range(mine):
         pair_one[i] = outer_row(mine + i)
 
-    depth = jnp.sum(bias_all[:, local, 0, :], axis=0, keepdims=True)
+    depth = jnp.sum(right_all[:, 0, local, :], axis=0, keepdims=True)
     depth_rows = jnp.transpose(jnp.broadcast_to(depth, (residues, residues)))
     lane = lax.broadcasted_iota(jnp.int32, (1, residues), 1)
     dead = jnp.where(lane % padded < local, masked_score, 3.0 * masked_score)
@@ -448,7 +446,7 @@
         live = depth > first_seq + s.astype(jnp.float32)
         seq_pad[:, :local, :] = seq_in[s]
         x = seq_pad[...].reshape(residues, seq_in.shape[3])
-        seq_res[s] = rows_attention(
+        result = rows_attention(
             x,
             lambda h: bias_all[:, :, h, :].reshape(residues, residues),
             lambda scores: jnp.where(live, scores, dead),
@@ -456,6 +454,7 @@
             row_out,
             heads,
         )
+        seq_res[s] = result.reshape(shares, padded, seq_in.shape[3])[:, :local, :]
 
     column_in[0] = depth_rows
     swap.wait()
@@ -484,11 +483,26 @@
     )
     own.start()
 
+    forward(pairs[1])
     each(1, shares, lambda k: seq_copy(k).wait())
-    each(0, per_seq // 2, row_sequence)
+    early = per_seq // 2
+    each(0, early, row_sequence)
+
+    def row_copy(k, late):
+        peer = (r + k) % shares
+        at, count = (early, per_seq - early) if late else (0, early)
+        return remote(
+            seq_res.at[pl.ds(at, count), peer],
+            msa_o.at[pl.ds(r * per_seq + at, count)],
+            out_send.at[late, k],
+            out_recv.at[late, k],
+            b,
+            peer,
+        )
 
     own.wait()
     each(1, everyone, lambda k: start_copy(k).wait())
+    each(1, shares, lambda k: row_copy(k, 0).start())
 
     for i in range(mine):
         two = rows_attention(
@@ -521,26 +535,13 @@
         tile_send.at[me], tile_all.at[pl.ds(my_rows, mine)], own_sem.at[0]
     )
     own.start()
-    each(per_seq // 2, per_seq, row_sequence)
-
-    def row_copy(k):
-        peer = (r + k) % shares
-        return remote(
-            seq_res.at[:, pl.ds(pl.multiple_of(peer * padded, padded), padded), :],
-            msa_o.at[pl.ds(r * per_seq, per_seq)],
-            out_send.at[k],
-            out_recv.at[k],
-            b,
-            peer,
-        )
+    each(early, per_seq, row_sequence)
 
     own.wait()
     each(1, everyone, lambda k: tile_copy(k).wait())
-    each(1, shares, lambda k: row_copy(k).start())
+    each(1, shares, lambda k: row_copy(k, 1).start())
     own_row = pltpu.make_async_copy(
-        seq_res.at[:, pl.ds(pl.multiple_of(r * padded, padded), padded), :],
-        msa_o.at[pl.ds(r * per_seq, per_seq)],
-        own_sem.at[1],
+        seq_res.at[:, r], msa_o.at[pl.ds(r * per_seq, per_seq)], own_sem.at[1]
     )
     own_row.start()
 
@@ -588,7 +589,8 @@
     own.start()
     own.wait()
     own_row.wait()
-    each(1, shares, lambda k: row_copy(k).wait())
+    each(1, shares, lambda k: row_copy(k, 0).wait())
+    each(1, shares, lambda k: row_copy(k, 1).wait())
     each(1, everyone, lambda k: pair_copy(k).wait())
 
 
@@ -636,7 +638,7 @@
     msa_o, pair_o = pl.pallas_call(
         functools.partial(block_kernel, local, branches, shares, heads, heads_z),
         out_shape=(
-            jax.ShapeDtypeStruct((part, padded, features), f32),
+            jax.ShapeDtypeStruct((part, local, features), f32),
             jax.ShapeDtypeStruct((everyone, padded, lanes), f32),
         ),
         in_specs=[vmem] * len(args),
@@ -650,7 +652,7 @@
             pltpu.VMEM((shares, half, padded, sequences), f32),
             pltpu.VMEM((shares, padded, heads, spread), f32),
             pltpu.VMEM((per_seq, shares, local, features), f32),
-            pltpu.VMEM((per_seq, spread, features), f32),
+            pltpu.VMEM((per_seq, shares, local, features), f32),
             pltpu.VMEM((mine, spread, width), f32),
             pltpu.VMEM((mine, spread, width), f32),
             pltpu.VMEM((mine, spread, width), f32),
@@ -669,8 +671,8 @@
             dma((2, 2, outers)),
             dma((shares,)),
             dma((shares,)),
-            dma((shares,)),
-            dma((shares,)),
+            dma((2, shares)),
+            dma((2, shares)),
             dma,
             dma,
             dma((everyone,)),
@@ -687,7 +689,7 @@
     piece = width // branches
     pair_o = pair_o[:, :local, : mine * piece].reshape(everyone, local, mine, piece)
     pair_o = jnp.transpose(pair_o, (1, 0, 2, 3)).reshape(local, residues, piece)
-    return msa_o[:, :local], pair_o
+    return msa_o, pair_o
 
 
 def per_device(
@@ -719,7 +721,7 @@
     mine = local // branches
     per_seq = sequences // everyone
     room = -(-(local + 1) // 8) * 8
-    if shares * room == width and shares % 4 == 0 and width == 128:
+    if shares * room == width == sequences == 128 and shares % 4 == 0:
         return fused(
             msa, pair, msa_mask, row_proj, row_out, row_bias_w, first_w, other_w, outer_w,
             start_proj, start_bias_w, start_out, end_proj, end_bias_w, end_out, room,

time: 90.4 us -> 82.5 us (0.913)
  Pallas kernels: 80.5 us -> 72.1 us
    pallas_call x1, Pallas kernels: 80.5 us -> 72.1 us  [fused(): pl.pallas_call(functools.partial(block_kernel, local, branches, shares, h...]
where the time goes in v4:
time: 82.5 us; the launch traced here: 81.8 us
  Pallas kernels  72.1 us (87%)
  local copies, waits for them, and re-layouts  7.59 us (9%)
  other arithmetic  1.33 us (2%)
    pallas_call x1, Pallas kernels, fused(): pl.pallas_call(functools.partial(block_kernel, local, branches, shares, h...  72.1 us
    unnamed x15, local copies, waits for them, and re-layouts  5.42 us

profile of v4, /device:TPU:0, one launch (start us, length us, event | category | flops | bytes accessed | tf_op | source)
XLA Modules:
  0.0 81.8 jit_solution(11556309884762075410)
XLA Ops:
  0.6 0.0 copy-start
  0.7 0.0 copy-start.4
  0.7 0.0 copy-start.3
  0.7 1.0 %copy-done = f32[1024,128]{1,0:T(8,128)S(1)} copy-done((f32[1024,128]{1,0:T(8,128)S(1)}, f32[1024,128]{1,0:T(8,128)}, u32[]{:S(2)}) %copy-start) | copy-done | bytes 524312
  1.7 0.0 copy-done.4
  1.7 0.1 convert_reduce_fusion
  1.8 0.1 dynamic_update_slice.3.place_ref
  2.0 0.0 copy-start.5
  2.0 0.6 convert_bitcast_fusion.mask_ref
  2.6 0.0 copy-done.5
  2.6 0.7 constant_dynamic-slice_fusion
  3.3 0.0 copy-done.3
  3.3 0.6 maximum_bitcast_fusion.factor_w
  3.9 0.0 copy-start.1
  3.9 0.1 copy.26
  4.0 0.8 %copy.28.outer_ref = f32[128,512]{1,0:T(8,128)} copy(f32[128,512]{0,1:T(8,128)S(1)} %bitcast.18) | data formatting | bytes 524288 | tf_op jit(solution)/shard_map/reshape | solution.py:625
  4.9 0.2 copy-done.1
  5.0 1.4 %copy.27.msa_ref = f32[128,6,256]{2,1,0:T(8,128)} copy(f32[128,6,256]{2,0,1:T(8,128)S(1)} %copy-done.1) | data formatting | bytes 1572864 | tf_op args[0]
  6.5 72.1 %shard_map.158 = (f32[64,6,256]{2,1,0:T(8,128)}, f32[32,8,256]{2,1,0:T(8,128)}) custom-call(f32[128,6,256]{2,1,0:T(8,128)} %copy.27.msa_ref, f32[6,128]{1,0:T(8,128)} %convert_bitcast_fusion.mask_ref, f32[6,96,128]{2,1,0:T(8,128)} %wide_ref.1, f32[1,128]{1,0:T(1,128)} %copy-done.5, f32[48,256]{1,0:T(8,128)} %maximum_bitcast_fusion.factor_w, ...), custom_call_target="tpu_custom_call" | custom-call | tf_op jit(solution)/shard_map/pallas_call | solution.py:638
  78.6 0.0 copy-start.2
  78.6 2.0 %copy.30 = f32[64,6,256]{2,0,1:T(8,128)} copy(f32[64,6,256]{2,1,0:T(8,128)} %get-tuple-element.10) | data formatting | bytes 786432
  80.6 0.0 copy-done.2
  80.6 0.1 copy.29
  80.7 0.2 reshape.18
  80.8 0.1 reshape.19
  81.0 0.8 copy.31
  (2 shorter events, 0.0 us)
Async XLA Ops:
  0.6 1.0 %copy-start = (f32[1024,128]{1,0:T(8,128)S(1)}, f32[1024,128]{1,0:T(8,128)}, u32[]{:S(2)}) copy-start(f32[1024,128]{1,0:T(8,128)} %param.24) | copy-start | bytes 1572868
  0.7 1.0 %copy-start.4 = (s32[128,6]{0,1:T(8,128)S(1)}, s32[128,6]{0,1:T(8,128)}, u32[]{:S(2)}) copy-start(s32[128,6]{0,1:T(8,128)} %param.18) | copy-start | bytes 9220
  0.7 2.6 %copy-start.3 = (f32[256,32]{0,1:T(8,128)S(1)}, f32[256,32]{0,1:T(8,128)}, u32[]{:S(2)}) copy-start(f32[256,32]{0,1:T(8,128)} %param.22) | copy-start | bytes 98308
  2.0 0.6 copy-start.5
  3.9 1.1 %copy-start.1 = (f32[128,6,256]{2,0,1:T(8,128)S(1)}, f32[128,6,256]{2,0,1:T(8,128)}, u32[]{:S(2)}) copy-start(f32[128,6,256]{2,0,1:T(8,128)} %param.16) | copy-start | bytes 2359300
  78.6 2.0 %copy-start.2 = (f32[32,8,256]{2,1,0:T(8,128)S(1)}, f32[32,8,256]{2,1,0:T(8,128)}, u32[]{:S(2)}) copy-start(f32[32,8,256]{2,1,0:T(8,128)} %get-tuple-element.5) | copy-start | bytes 786436
